TPU v7x, 32 devices: a whole 2x2x4 slice. The times are simulated.
32 devices in a mesh: section: 2 (over x), dp: 4 (over y, core), shard: 4 (over z).
Axes of the slice: x: 2, y: 2, z: 4, core: 2. Of those that a mesh axis runs over, the one named last changes fastest.
Arguments:
- norm_input: bfloat16 [2, 4, 512, 3584], P('section', 'dp', 'shard'), may hold values from -6 to 6
- norm_gain: float32 [2, 3584], P('section'), may hold values from 0.1 to 1.9
- branch_grad: bfloat16 [2, 4, 512, 3584], P('section', 'dp', 'shard'), may hold values from -6 to 6
- residual_grad: bfloat16 [2, 4, 512, 3584], P('section', 'dp', 'shard'), may hold values from -6 to 6
- down_weight: bfloat16 [2, 1792, 3584], P('section', 'shard'), may hold values from -0.09375 to 0.09375
Outputs:
- boundary_grad: bfloat16 [2, 4, 512, 3584], P('section', 'dp', 'shard')
- gain_grad: float32 [2, 3584], P('section')
- unit_grads: bfloat16 [2, 4, 512, 1792], P('section', 'dp', None, 'shard')
All inputs are finite; a program needn't handle non-finite values.
Results may differ from a plain program's by a relative error of at most 0.0049.
Values may be sent and summed in bfloat16 or wider, within the bound.
No kernel may reach another device: no remote copies, remote signals or barrier semaphores. Data moves between devices by JAX's collectives and lax.ppermute only.
A program may use at most 128 MiB of HBM per device.

v0:
```python
import jax
import jax.numpy as jnp
from jax import lax
from jax.sharding import PartitionSpec as P

epsilon = 1e-05


def from_partner(block, axis, distance):
    count = lax.axis_size(axis)
    route = []
    for low in range(count):
        high = low | 1 << distance
        if high != low and high < count:
            route += [(low, high), (high, low)]
    return lax.ppermute(block, axis, route)


def norm_backward(inputs, gain_row, branch, residual):
    values = inputs.astype(jnp.float32)
    inverse = lax.rsqrt(jnp.mean(values * values, axis=-1, keepdims=True) + epsilon)
    normed = values * inverse
    upstream = branch.astype(jnp.float32)
    scaled = upstream * gain_row
    project = jnp.mean(scaled * normed, axis=-1, keepdims=True)
    boundary = (residual.astype(jnp.float32) + inverse * (scaled - normed * project)).astype(
        jnp.bfloat16
    )
    return (boundary, jnp.sum(upstream * normed, axis=0))


def per_device(norm_input, norm_gain, branch_grad, residual_grad, down_weight):
    weight = down_weight[0]
    boundary, gain_part = norm_backward(
        norm_input[0, 0], norm_gain[0], branch_grad[0, 0], residual_grad[0, 0]
    )
    gain_total = lax.psum(gain_part, ("dp", "shard"))
    arrived = from_partner(boundary, "section", 0)
    fresh = jnp.einsum(
        "nd,hd->nh",
        lax.all_gather(arrived, "shard", axis=0, tiled=True),
        weight,
        preferred_element_type=jnp.float32,
    ).astype(jnp.bfloat16)
    gain_grad = gain_total / fresh.shape[0]
    return (boundary[None, None], gain_grad[None], fresh[None, None])


def solution(mesh):
    in_specs = (
        P("section", "dp", "shard", None),
        P("section", None),
        P("section", "dp", "shard", None),
        P("section", "dp", "shard", None),
        P("section", "shard", None),
    )
    out_specs = (
        P("section", "dp", "shard", None),
        P("section", None),
        P("section", "dp", None, "shard"),
    )
    return jax.shard_map(
        per_device, mesh=mesh, in_specs=in_specs, out_specs=out_specs, check_vma=False
    )
```

profile of v0, /device:TPU:0, one launch (start us, length us, event | category | flops | bytes accessed | tf_op | source)
XLA Modules:
  0.0 124.3 jit_solution(13056092818408830644)
XLA Ops:
  7.2 0.0 copy-start
  7.2 0.0 all-gather.2.cloned.1.call-start
  7.2 1.6 %fusion.17 = f32[128]{0:T(128)S(1)} fusion(bf16[1,1,128,3584]{3,2,1,0:T(8,128)(2,1)} %param.5), kind=kLoop, calls=%fused_computation.23 | loop fusion | flops 1376128 | bytes 918016 | tf_op jit(solution)/shard_map/reduce_sum | solution.py:21
  8.8 0.8 reduce
  9.6 0.0 copy-start.1
  9.6 0.0 copy-start.2
  9.6 2.3 %fusion.16 = (f32[3584]{0:T(1024)S(1)}, f32[128]{0:T(128)S(1)}) fusion(bf16[1,1,128,3584]{3,2,1,0:T(8,128)(2,1)} %param.5, bf16[1,1,128,3584]{3,2,1,0:T(8,128)(2,1)} %param.7, f32[128]{0:T(128)S(1)} %add_rsqrt_fusion, f32[3584]{0:T(1024)S(1)} %reduce), kind=kLoop, calls=%fused_computation.22 | loop fusion | flops 3666304 | bytes 1864704 | tf_op jit(solution)/shard_map/reduce_sum | solution.py:29
  11.9 0.0 copy-done.1
  11.9 0.0 copy-done.2
  12.0 1.8 %fusion.11 = bf16[128,3584]{1,0:T(8,128)(2,1)S(1)} fusion(bf16[1,1,128,3584]{3,2,1,0:T(8,128)(2,1)S(1)} %copy-done.2, bf16[1,1,128,3584]{3,2,1,0:T(8,128)(2,1)} %param.8, bf16[1,1,128,3584]{3,2,1,0:T(8,128)(2,1)S(1)} %copy-done.1, f32[128]{0:T(128)S(1)} %broadcast_multiply_fusion.1, f32[128]{0:T(128)S(1)} %add_rsqrt_fusion, f32[3584]{0:T(1024)S(1)} %reduce), kind=kLoop, calls=%fused_computation.17 | loop fusion | flops 4587520 | bytes 3685376 | tf_op jit(solution)/shard_map/convert_element_type | solution.py:26
  13.8 3.0 %collective-permute-start = (bf16[128,3584]{1,0:T(8,128)(2,1)S(1)}, bf16[128,3584]{1,0:T(8,128)(2,1)}, u32[]{:S(2)}, u32[]{:S(2)}) collective-permute-start(bf16[128,3584]{1,0:T(8,128)(2,1)S(1)} %fusion.11), channel_id=1, source_target_pairs={{0,16},{16,0},{1,17},{17,1},{2,18},{18,2},{3,19},{19,3},{4,20},{20... | collective-permute-start | bytes 2752520 | tf_op jit(solution)/shard_map/ppermute | solution.py:16
  16.8 20.5 %collective-permute-done = bf16[128,3584]{1,0:T(8,128)(2,1)} collective-permute-done((bf16[128,3584]{1,0:T(8,128)(2,1)S(1)}, bf16[128,3584]{1,0:T(8,128)(2,1)}, u32[]{:S(2)}, u32[]{:S(2)}) %collective-permute-start) | collective-permute-done | bytes 917536 | tf_op jit(solution)/shard_map/ppermute | solution.py:16
  37.3 0.0 all-gather.2.cloned.1.call-update
  37.3 65.9 %psum.7 = f32[3584]{0:T(1024)S(1)} all-reduce(f32[3584]{0:T(1024)S(1)} %get-tuple-element.3), channel_id=1, replica_groups=mesh['section'=2,'dp'=4,'shard'=4] {'dp','shard'}, use_global_device_ids=true, to_apply=%region_3.0 | all-reduce | flops 3584 | bytes 28672 | tf_op jit(solution)/shard_map/psum | solution.py:37
  103.2 0.6 broadcast_in_dim.4
  103.8 3.3 %fusion.12 = bf16[1,1,128,3584]{3,2,1,0:T(8,128)(2,1)} fusion(bf16[1,1,128,3584]{3,2,1,0:T(8,128)(2,1)} %param.8, bf16[1,1,128,3584]{3,2,1,0:T(8,128)(2,1)} %param.7, bf16[1,1,128,3584]{3,2,1,0:T(8,128)(2,1)} %param.5, f32[128]{0:T(128)S(1)} %broadcast_multiply_fusion.1, f32[3584]{0:T(1024)S(1)} %reduce, f32[128]{0:T(128)S(1)} %add_rsqrt_fusion), kind=kLoop, calls=%fused_computation.18 | loop fusion | flops 4587520 | bytes 3685376 | tf_op jit(solution)/shard_map/convert_element_type | solution.py:26
  107.1 5.7 %all-gather.2.cloned.1.call-done = bf16[512,3584]{1,0:T(8,128)(2,1)} async-done(((bf16[128,3584]{1,0:T(8,128)(2,1)}), bf16[512,3584]{1,0:T(8,128)(2,1)}) %all-gather.2.cloned.1.call-update) | async-done | bytes 3670032 | tf_op jit(solution)/shard_map/all_gather | solution.py:41
  112.8 0.0 copy-done
  112.8 4.7 %fusion.22 = bf16[1,1,512,448]{2,3,1,0:T(8,128)(2,1)} fusion(bf16[512,3584]{1,0:T(8,128)(2,1)} %all-gather.2.cloned.1.call-done, bf16[1,448,3584]{2,1,0:T(8,128)(2,1)S(1)} %copy-done), kind=kOutput, calls=%fused_computation.26 | convolution fusion | flops 1644396544 | bytes 7340032 | tf_op jit(solution)/shard_map/nd,hd->nh/dot_general | solution.py:39
  (3 shorter events, 0.0 us)
Async XLA Ops:
  7.2 105.7 %copy-start = (bf16[1,448,3584]{2,1,0:T(8,128)(2,1)S(1)}, bf16[1,448,3584]{2,1,0:T(8,128)(2,1)}, u32[]{:S(2)}) copy-start(bf16[1,448,3584]{2,1,0:T(8,128)(2,1)} %param.9) | copy-start | bytes 9633796
  7.2 105.6 %all-gather.2.cloned.1.call-start = ((), (), s32[]{:S(2)}) async-start(), calls=%async_computation | async-start | bytes 4587520 | tf_op jit(solution)/shard_map/all_gather | solution.py:41
  9.6 2.3 %copy-start.1 = (bf16[1,1,128,3584]{3,2,1,0:T(8,128)(2,1)S(1)}, bf16[1,1,128,3584]{3,2,1,0:T(8,128)(2,1)}, u32[]{:S(2)}) copy-start(bf16[1,1,128,3584]{3,2,1,0:T(8,128)(2,1)} %param.5) | copy-start | bytes 2752516
  9.6 2.3 %copy-start.2 = (bf16[1,1,128,3584]{3,2,1,0:T(8,128)(2,1)S(1)}, bf16[1,1,128,3584]{3,2,1,0:T(8,128)(2,1)}, u32[]{:S(2)}) copy-start(bf16[1,1,128,3584]{3,2,1,0:T(8,128)(2,1)} %param.7) | copy-start | bytes 2752516
  13.8 23.5 %collective-permute-start = (bf16[128,3584]{1,0:T(8,128)(2,1)S(1)}, bf16[128,3584]{1,0:T(8,128)(2,1)}, u32[]{:S(2)}, u32[]{:S(2)}) collective-permute-start(bf16[128,3584]{1,0:T(8,128)(2,1)S(1)} %fusion.11), channel_id=1, source_target_pairs={{0,16},{16,0},{1,17},{17,1},{2,18},{18,2},{3,19},{19,3},{4,20},{20... | collective-permute-start | bytes 2752520 | tf_op jit(solution)/shard_map/ppermute | solution.py:16
Sparse Core Ops, SparseCore 0:
  37.4 75.3 all-gather.1
where the time goes:
time: 125 us; the launch traced here: 124 us
  blocking collectives  65.9 us (53%)
  waiting for transfers between devices  26.2 us (21%)
  between operations  14.1 us (11%)
  other arithmetic  9.79 us (8%)
  matrix products  4.65 us (4%)
  starting transfers between devices  3.07 us (2%)
    psum x1, blocking collectives, per_device(): gain_total = lax.psum(gain_part, ('dp', 'shard'))  65.9 us
    ppermute x1, waiting for transfers between devices, from_partner(): return lax.ppermute(block, axis, route)  20.5 us
    all_gather x1, waiting for transfers between devices, per_device(): lax.all_gather(arrived, 'shard', axis=0, tiled=True)  5.7 us
    convert_element_type x2, other arithmetic, norm_backward(): (residual.astype(jnp.float32) + inverse * (scaled - normed * project)).as...  5.11 us
    dot_general x1, matrix products, per_device(): jnp.einsum('nd,hd->nh', lax.all_gather(arrived, 'shard', axis=0, tiled=Tr...  4.65 us
    ppermute x1, starting transfers between devices, from_partner(): return lax.ppermute(block, axis, route)  3.03 us
  transfers between devices with their start and end apart: 2, of which 2 were waited for; matrix products, arithmetic and copies ran while one was open for 3% of the time, Pallas kernels for 0%

commit v1 on v0

v1 whole, which is shorter than its diff:
```python
import functools
import math

import jax
import jax.numpy as jnp
from jax import lax
from jax.experimental import pallas as pl
from jax.experimental.pallas import tpu as pltpu
from jax.sharding import PartitionSpec as P

epsilon = 1e-05


def norm_kernel(width, group, x_ref, gain_ref, up_ref, res_ref, out_ref, lo_ref, hi_ref, sum_ref, part_ref):
    rows, dim = x_ref.shape
    half = lo_ref.shape[1]
    f32 = jnp.float32

    @pl.when(pl.program_id(0) == 0)
    def _():
        part_ref[...] = jnp.zeros_like(part_ref)

    @pl.loop(0, rows // group)
    def _(step):
        here = pl.ds(pl.multiple_of(step * group, group), group)
        squares = jnp.zeros((group, 128), f32)
        cross = jnp.zeros((group, 128), f32)
        for at in range(0, dim, width):
            cols = slice(at, at + width)
            v = x_ref[here, cols].astype(f32)
            s = up_ref[here, cols].astype(f32) * gain_ref[:, cols]
            vv, sv = v * v, s * v
            for lane in range(0, width, 128):
                squares += vv[:, lane : lane + 128]
                cross += sv[:, lane : lane + 128]
        inverse = lax.rsqrt(jnp.sum(squares, axis=-1, keepdims=True) / dim + epsilon)
        project = inverse * (jnp.sum(cross, axis=-1, keepdims=True) / dim)
        for at in range(0, dim, width):
            cols = slice(at, at + width)
            u = up_ref[here, cols].astype(f32)
            normed = x_ref[here, cols].astype(f32) * inverse
            moved = inverse * (u * gain_ref[:, cols] - normed * project)
            b = (res_ref[here, cols].astype(f32) + moved).astype(jnp.bfloat16)
            out_ref[here, cols] = b
            if at < half:
                lo_ref[here, cols] = b
            else:
                hi_ref[here, at - half : at - half + width] = b
            terms = u * normed
            part_ref[:, cols] += functools.reduce(jnp.add, [terms[at : at + 8] for at in range(0, group, 8)])

    @pl.when(pl.program_id(0) == pl.num_programs(0) - 1)
    def _():
        sum_ref[...] = jnp.sum(part_ref[...], axis=0, keepdims=True)


def norm_backward(x, gain, up, res):
    rows, dim = x.shape
    half = dim // 2
    block = math.gcd(rows, 64)
    span = lambda cols: pl.BlockSpec((block, cols), lambda i: (i, 0))
    row = pl.BlockSpec((1, dim), lambda i: (0, 0))
    shape = jax.ShapeDtypeStruct
    return pl.pallas_call(
        functools.partial(norm_kernel, math.gcd(half, 256), math.gcd(block, 32)),
        grid=(rows // block,),
        in_specs=[span(dim), row, span(dim), span(dim)],
        out_specs=[span(dim), span(half), span(half), row],
        out_shape=[
            shape((rows, dim), jnp.bfloat16),
            shape((rows, half), jnp.bfloat16),
            shape((rows, half), jnp.bfloat16),
            shape((1, dim), jnp.float32),
        ],
        scratch_shapes=[pltpu.VMEM((8, dim), jnp.float32)],
        cost_estimate=pl.CostEstimate(flops=12 * rows * dim, bytes_accessed=10 * rows * dim, transcendentals=rows),
        name="norm_backward",
    )(x, gain, up, res)


def dot(w, t):
    return lax.dot_general(w, t, (((1,), (1,)), ((), ())), preferred_element_type=jnp.float32)


def swap(axis, distance):
    count = lax.axis_size(axis)
    return [(at, at ^ distance) for at in range(count)]


def send(block, axis, route):
    return lax.ppermute(block, axis, route)


def relay(norm_input, norm_gain, branch_grad, residual_grad, down_weight):
    weight = down_weight[0]
    hidden, dim = weight.shape
    copies = lax.axis_size("dp")
    me_dp, me = lax.axis_index("dp"), lax.axis_index("shard")
    last = lax.axis_size("shard") - 1
    flip = lambda at: last - at
    both = lambda route: route + [(flip(a), flip(b)) for a, b in route]
    inward, across, outward = both([(0, 1)]), both([(1, 2)]), both([(1, 0)])
    count = last + 1
    cross = lambda route: [((1 - g) * count + a, g * count + b) for g in (0, 1) for a, b in route]
    other = ("section", "shard")

    part = hidden // copies
    piece = lax.dynamic_slice_in_dim(weight, me_dp * part, part, axis=0)
    pieces = [send(piece, "shard", inward)]
    boundary, lo, hi, gain = norm_backward(norm_input[0, 0], norm_gain, branch_grad[0, 0], residual_grad[0, 0])

    ends = cross(both([(0, 0)]))
    outer_lo = send(lo, other, ends)
    far = send(boundary, other, cross(across))
    outer_hi = send(hi, other, ends)

    distance = 1
    while distance < copies:
        gain = gain + send(gain, "dp", swap("dp", distance))
        distance *= 2
    edge_lo = send(outer_lo, "shard", inward)
    summed = [send(gain, "shard", inward), send(gain, "shard", both([(0, 2)])), send(gain, "shard", across)]
    gain = functools.reduce(jnp.add, summed, gain)
    edge_hi = send(outer_hi, "shard", inward)

    distance = copies // 2
    orders = [0]
    while distance:
        pieces = pieces + [send(p, "dp", swap("dp", distance)) for p in pieces]
        orders = orders + [at ^ distance for at in orders]
        distance //= 2
    edge_weight = jnp.concatenate([p for _, p in sorted(zip(orders, pieces), key=lambda t: t[0])])

    gain_out = send(gain, "shard", outward)
    near = send(boundary, other, cross(both([(1, 1)])))
    tail_lo = send(edge_lo, "shard", across)
    tail_hi = send(edge_hi, "shard", across)

    rows, half = lo.shape
    bf16 = jnp.bfloat16
    low, high = slice(0, half), slice(half, dim)
    own, edge = {}, {}
    own["far"] = dot(weight, far).astype(bf16)
    own_half = dot(weight[:, low], edge_lo)
    edge["far"] = dot(edge_weight, far).astype(bf16)
    edge["edge"] = (dot(edge_weight[:, low], edge_lo) + dot(edge_weight[:, high], edge_hi)).astype(bf16)
    early = jnp.concatenate([edge["far"], edge["edge"]], axis=1)
    one = send(early, "shard", outward)
    near, edge_hi, early = lax.optimization_barrier((near, edge_hi, early))
    edge["near"] = dot(edge_weight, near).astype(bf16)
    two = send(edge["near"], "shard", outward)
    begun = dot(edge_weight[:, low], tail_lo)
    own["edge"] = (own_half + dot(weight[:, high], edge_hi)).astype(bf16)
    tail_hi, own["far"], own["edge"], begun = lax.optimization_barrier((tail_hi, own["far"], own["edge"], begun))
    edge["tail"] = (begun + dot(edge_weight[:, high], tail_hi)).astype(bf16)
    three = send(edge["tail"], "shard", outward)
    tail_lo, tail_hi, near, _ = lax.optimization_barrier((tail_lo, tail_hi, near, edge["tail"]))
    own["near"] = dot(weight, near).astype(bf16)
    own["tail"] = (dot(weight[:, low], tail_lo) + dot(weight[:, high], tail_hi)).astype(bf16)
    one, two, own["near"], own["tail"] = lax.optimization_barrier((one, two, own["near"], own["tail"]))
    inner = (me != 0) & (me != last)
    gain_grad = jnp.where(inner, gain, gain_out) / (rows * count)

    def restore(block):
        block = block.reshape(copies, part, rows)
        distance = 1
        while distance < copies:
            order = [at ^ distance for at in range(copies)]
            moved = jnp.stack([block[at] for at in order])
            block = jnp.where((me_dp & distance) != 0, moved, block)
            distance *= 2
        return block.reshape(hidden, rows)

    got = {"far": one[:, :rows], "edge": one[:, rows:], "near": two}
    result = {name: jnp.where(inner, own[name], restore(got[name])) for name in got}
    names = tuple(result)
    ready = lax.optimization_barrier((three, own["tail"], gain_grad) + tuple(result[name] for name in names))
    three, own["tail"], gain_grad = ready[:3]
    result = dict(zip(names, ready[3:]))
    result["tail"] = jnp.where(inner, own["tail"], restore(three))
    up = jnp.concatenate([result[name] for name in ("edge", "near", "far", "tail")], axis=1)
    down = jnp.concatenate([result[name] for name in ("tail", "far", "near", "edge")], axis=1)
    fresh = jnp.where(me < count // 2, up, down).T
    return (boundary[None, None], gain_grad, fresh[None, None])


def gather(norm_input, norm_gain, branch_grad, residual_grad, down_weight):
    boundary, _, _, gain = norm_backward(norm_input[0, 0], norm_gain, branch_grad[0, 0], residual_grad[0, 0])
    arrived = lax.ppermute(boundary, "section", swap("section", 1))
    fresh = jnp.einsum(
        "nd,hd->nh",
        lax.all_gather(arrived, "shard", axis=0, tiled=True),
        down_weight[0],
        preferred_element_type=jnp.float32,
    ).astype(jnp.bfloat16)
    gain_grad = lax.psum(gain, ("dp", "shard")) / fresh.shape[0]
    return (boundary[None, None], gain_grad, fresh[None, None])


def solution(mesh):
    in_specs = (
        P("section", "dp", "shard", None),
        P("section", None),
        P("section", "dp", "shard", None),
        P("section", "dp", "shard", None),
        P("section", "shard", None),
    )
    out_specs = (
        P("section", "dp", "shard", None),
        P("section", None),
        P("section", "dp", None, "shard"),
    )
    line = mesh.shape["shard"] == 4 and mesh.shape["section"] == 2
    mapped = functools.partial(jax.shard_map, mesh=mesh, in_specs=in_specs, out_specs=out_specs, check_vma=False)
    if not line:
        return mapped(gather)
    return mapped(relay)
```

time: 125 us -> 95.8 us (0.77)
  blocking collectives: 65.9 us -> 0 us
  starting transfers between devices: 3.07 us -> 34.8 us
  between operations: 14.1 us -> 1.08 us
  waiting for transfers between devices: 26.2 us -> 38.4 us
  other arithmetic: 9.79 us -> 2.71 us
  matrix products: 4.65 us -> 10.9 us
  Pallas kernels: 0 us -> 3.71 us
  local copies, waits for them, and re-layouts: 0.63 us -> 3.6 us
    psum x1 -> x0, blocking collectives: 65.9 us -> none  [per_device(): gain_total = lax.psum(gain_part, ('dp', 'shard'))]
    ppermute x1 -> x21, starting transfers between devices: 3.03 us -> 34.8 us  [send(): return lax.ppermute(block, axis, route)]
    ppermute x1 -> x21, waiting for transfers between devices: 20.5 us -> 38.4 us  [send(): return lax.ppermute(block, axis, route)]
    dot_general x1 -> x12, matrix products: 4.65 us -> 10.9 us  [dot(): lax.dot_general(w, t, (((1,), (1,)), ((), ())), preferred_element_type=jn...]
    all_gather x1 -> x0, waiting for transfers between devices: 5.7 us -> none  [per_device(): lax.all_gather(arrived, 'shard', axis=0, tiled=True)]
    convert_element_type x2 -> x1, other arithmetic: 5.11 us -> 0.03 us  [relay(): edge['tail'] = (begun + dot(edge_weight[:, high], tail_hi)).astype(bf16)]
    reduce_sum x2 -> x0, other arithmetic: 3.91 us -> none  [the longest x1 2.31 us: norm_backward(): return (boundary, jnp.sum(upstream * normed, axis=0))]
    pallas_call x0 -> x1, Pallas kernels: none -> 3.71 us  [norm_backward(): pl.pallas_call(functools.partial(norm_kernel, math.gcd(half, 256), math.g...]
  transfers between devices with their start and end apart: 2 -> 21, of which waited for: 2 -> 10; matrix products, arithmetic and copies ran while one was open for 3% -> 16% of each run, Pallas kernels for 0% -> 0%
where the time goes in v1:
time: 95.8 us; the launch traced here: 95.2 us
  waiting for transfers between devices  38.4 us (40%)
  starting transfers between devices  34.8 us (36%)
  matrix products  10.9 us (11%)
  Pallas kernels  3.71 us (4%)
  local copies, waits for them, and re-layouts  3.6 us (4%)
  other arithmetic  2.71 us (3%)
  between operations  1.08 us (1%)
    ppermute x21, waiting for transfers between devices, send(): return lax.ppermute(block, axis, route)  38.4 us
    ppermute x21, starting transfers between devices, send(): return lax.ppermute(block, axis, route)  34.8 us
    dot_general x12, matrix products, dot(): lax.dot_general(w, t, (((1,), (1,)), ((), ())), preferred_element_type=jn...  10.9 us
    pallas_call x1, Pallas kernels, norm_backward(): pl.pallas_call(functools.partial(norm_kernel, math.gcd(half, 256), math.g...  3.71 us
    dynamic_slice x1, local copies, waits for them, and re-layouts, relay(): piece = lax.dynamic_slice_in_dim(weight, me_dp * part, part, axis=0)  2.1 us
  transfers between devices with their start and end apart: 21, of which 10 were waited for; matrix products, arithmetic and copies ran while one was open for 16% of the time, Pallas kernels for 0%

profile of v1, /device:TPU:0, one launch (start us, length us, event | category | flops | bytes accessed | tf_op | source)
XLA Modules:
  0.0 95.2 jit_solution(14646666231163030604)
XLA Ops:
  0.6 3.7 %norm_backward.1 = (bf16[128,3584]{1,0:T(8,128)(2,1)}, bf16[128,1792]{1,0:T(8,128)(2,1)}, bf16[128,1792]{1,0:T(8,128)(2,1)}, f32[1,3584]{1,0:T(1,128)}) custom-call(bf16[128,3584]{1,0:T(8,128)(2,1)} %bitcast.111, f32[1,3584]{1,0:T(1,128)} %gain_ref.1, bf16[128,3584]{1,0:T(8,128)(2,1)} %bitcast.112, bf16[128,3584]{1,0:T(8,128)(2,1)} %bitcast.113), custom_call_target="tpu_custom_call" | custom-call | flops 5505024 | bytes 4587520 | tf_op jit(solution)/shard_map/norm_backward/pallas_call | solution.py:64
  4.9 1.0 %collective-permute-done.15 = f32[1,3584]{1,0:T(1,128)S(1)} collective-permute-done((f32[1,3584]{1,0:T(1,128)}, f32[1,3584]{1,0:T(1,128)S(1)}, u32[]{:S(2)}, u32[]{:S(2)}) %collective-permute-start.15) | collective-permute-done | bytes 14368 | tf_op jit(solution)/shard_map/ppermute | solution.py:91
  6.0 0.7 add.37
  6.7 2.9 %collective-permute-start.16 = (f32[1,3584]{1,0:T(1,128)S(1)}, f32[1,3584]{1,0:T(1,128)S(1)}, u32[]{:S(2)}, u32[]{:S(2)}) collective-permute-start(f32[1,3584]{1,0:T(1,128)S(1)} %add.37), channel_id=1, source_target_pairs={{0,8},{4,12},{8,0},{12,4},{1,9},{5,13},{9,1},{13,5},{2,10},{6,14},... | collective-permute-start | bytes 43016 | tf_op jit(solution)/shard_map/ppermute | solution.py:91
  9.6 1.7 %collective-permute-done.16 = f32[1,3584]{1,0:T(1,128)S(1)} collective-permute-done((f32[1,3584]{1,0:T(1,128)S(1)}, f32[1,3584]{1,0:T(1,128)S(1)}, u32[]{:S(2)}, u32[]{:S(2)}) %collective-permute-start.16) | collective-permute-done | bytes 14368 | tf_op jit(solution)/shard_map/ppermute | solution.py:91
  11.3 4.0 %collective-permute-start.17 = (f32[1,3584]{1,0:T(1,128)S(1)}, f32[1,3584]{1,0:T(1,128)S(1)}, u32[]{:S(2)}, u32[]{:S(2)}) collective-permute-start(f32[1,3584]{1,0:T(1,128)S(1)} %add.38), channel_id=1, source_target_pairs={{0,1},{3,2},{4,5},{7,6},{8,9},{11,10},{12,13},{15,14},{16,17},{19,... | collective-permute-start | bytes 43016 | tf_op jit(solution)/shard_map/ppermute | solution.py:91
  15.3 2.3 %collective-permute-start.18 = (f32[1,3584]{1,0:T(1,128)S(1)}, f32[1,3584]{1,0:T(1,128)S(1)}, u32[]{:S(2)}, u32[]{:S(2)}) collective-permute-start(f32[1,3584]{1,0:T(1,128)S(1)} %add.38), channel_id=1, source_target_pairs={{0,2},{3,1},{4,6},{7,5},{8,10},{11,9},{12,14},{15,13},{16,18},{19,... | collective-permute-start | bytes 43016 | tf_op jit(solution)/shard_map/ppermute | solution.py:91
  19.1 1.3 %collective-permute-start.20 = (f32[1,3584]{1,0:T(1,128)S(1)}, f32[1,3584]{1,0:T(1,128)S(1)}, u32[]{:S(2)}, u32[]{:S(2)}) collective-permute-start(f32[1,3584]{1,0:T(1,128)S(1)} %add_add_fusion), channel_id=1, source_target_pairs={{1,0},{2,3},{5,4},{6,7},{9,8},{10,11},{13,12},{14,15},{17,16},{18,... | collective-permute-start | bytes 43016 | tf_op jit(solution)/shard_map/ppermute | solution.py:91
  20.4 2.1 %dynamic-slice_bitcast_fusion = bf16[112,3584]{1,0:T(8,128)(2,1)} fusion(bf16[1,448,3584]{2,1,0:T(8,128)(2,1)} %param.9, s32[]{:T(128)S(6)} %select_n.95), kind=kLoop, calls=%fused_computation.30 | loop fusion | bytes 1605636 | tf_op jit(solution)/shard_map/dynamic_slice | solution.py:108
  22.5 5.4 %collective-permute-start.7 = (bf16[112,3584]{1,0:T(8,128)(2,1)}, bf16[112,3584]{1,0:T(8,128)(2,1)}, u32[]{:S(2)}, u32[]{:S(2)}) collective-permute-start(bf16[112,3584]{1,0:T(8,128)(2,1)} %dynamic-slice_bitcast_fusion), channel_id=1, source_target_pairs={{0,1},{3,2},{4,5},{7,6},{8,9},{11,10},{12,13},{15,14},{16,17},{19,... | collective-permute-start | bytes 2408456 | tf_op jit(solution)/shard_map/ppermute | solution.py:91
  27.9 3.4 %collective-permute-start = (bf16[128,1792]{1,0:T(8,128)(2,1)}, bf16[128,1792]{1,0:T(8,128)(2,1)}, u32[]{:S(2)}, u32[]{:S(2)}) collective-permute-start(bf16[128,1792]{1,0:T(8,128)(2,1)} %get-tuple-element.27), channel_id=1, source_target_pairs={{16,0},{19,3},{0,16},{3,19},{20,4},{23,7},{4,20},{7,23},{24,8},{27... | collective-permute-start | bytes 1376264 | tf_op jit(solution)/shard_map/ppermute | solution.py:91
  31.3 2.4 %collective-permute-start.4 = (bf16[128,1792]{1,0:T(8,128)(2,1)}, bf16[128,1792]{1,0:T(8,128)(2,1)}, u32[]{:S(2)}, u32[]{:S(2)}) collective-permute-start(bf16[128,1792]{1,0:T(8,128)(2,1)} %get-tuple-element.28), channel_id=1, source_target_pairs={{16,0},{19,3},{0,16},{3,19},{20,4},{23,7},{4,20},{7,23},{24,8},{27... | collective-permute-start | bytes 1376264 | tf_op jit(solution)/shard_map/ppermute | solution.py:91
  33.7 1.6 %collective-permute-start.3 = (bf16[128,3584]{1,0:T(8,128)(2,1)}, bf16[128,3584]{1,0:T(8,128)(2,1)}, u32[]{:S(2)}, u32[]{:S(2)}) collective-permute-start(bf16[128,3584]{1,0:T(8,128)(2,1)} %get-tuple-element.26), channel_id=1, source_target_pairs={{17,2},{18,1},{1,18},{2,17},{21,6},{22,5},{5,22},{6,21},{25,10},{2... | collective-permute-start | bytes 2752520 | tf_op jit(solution)/shard_map/ppermute | solution.py:91
  36.0 7.5 %collective-permute-done = bf16[128,1792]{1,0:T(8,128)(2,1)} collective-permute-done((bf16[128,1792]{1,0:T(8,128)(2,1)}, bf16[128,1792]{1,0:T(8,128)(2,1)}, u32[]{:S(2)}, u32[]{:S(2)}) %collective-permute-start) | collective-permute-done | bytes 458784 | tf_op jit(solution)/shard_map/ppermute | solution.py:91
  43.5 1.3 %collective-permute-start.1 = (bf16[128,1792]{1,0:T(8,128)(2,1)}, bf16[128,1792]{1,0:T(8,128)(2,1)S(1)}, u32[]{:S(2)}, u32[]{:S(2)}) collective-permute-start(bf16[128,1792]{1,0:T(8,128)(2,1)} %collective-permute-done), channel_id=1, source_target_pairs={{0,1},{3,2},{4,5},{7,6},{8,9},{11,10},{12,13},{15,14},{16,17},{19,... | collective-permute-start | bytes 1376264 | tf_op jit(solution)/shard_map/ppermute | solution.py:91
  44.8 5.2 %collective-permute-done.4 = bf16[128,1792]{1,0:T(8,128)(2,1)} collective-permute-done((bf16[128,1792]{1,0:T(8,128)(2,1)}, bf16[128,1792]{1,0:T(8,128)(2,1)}, u32[]{:S(2)}, u32[]{:S(2)}) %collective-permute-start.4) | collective-permute-done | bytes 458784 | tf_op jit(solution)/shard_map/ppermute | solution.py:91
  49.9 1.3 %collective-permute-start.5 = (bf16[128,1792]{1,0:T(8,128)(2,1)}, bf16[128,1792]{1,0:T(8,128)(2,1)S(1)}, u32[]{:S(2)}, u32[]{:S(2)}) collective-permute-start(bf16[128,1792]{1,0:T(8,128)(2,1)} %collective-permute-done.4), channel_id=1, source_target_pairs={{0,1},{3,2},{4,5},{7,6},{8,9},{11,10},{12,13},{15,14},{16,17},{19,... | collective-permute-start | bytes 1376264 | tf_op jit(solution)/shard_map/ppermute | solution.py:91
  51.3 1.6 %collective-permute-start.9 = (bf16[112,3584]{1,0:T(8,128)(2,1)}, bf16[112,3584]{1,0:T(8,128)(2,1)S(1)}, u32[]{:S(2)}, u32[]{:S(2)}) collective-permute-start(bf16[112,3584]{1,0:T(8,128)(2,1)} %collective-permute-done.7), channel_id=1, source_target_pairs={{0,8},{4,12},{8,0},{12,4},{1,9},{5,13},{9,1},{13,5},{2,10},{6,14},... | collective-permute-start | bytes 2408456 | tf_op jit(solution)/shard_map/ppermute | solution.py:91
  52.9 1.2 %constant_dynamic-update-slice_fusion.3 = bf16[448,3584]{1,0:T(8,128)(2,1)S(1)} fusion(bf16[112,3584]{1,0:T(8,128)(2,1)} %collective-permute-done.7), kind=kLoop, calls=%fused_computation.81 | loop fusion | bytes 1605632
  54.2 1.8 %collective-permute-done.1 = bf16[128,1792]{1,0:T(8,128)(2,1)S(1)} collective-permute-done((bf16[128,1792]{1,0:T(8,128)(2,1)}, bf16[128,1792]{1,0:T(8,128)(2,1)S(1)}, u32[]{:S(2)}, u32[]{:S(2)}) %collective-permute-start.1) | collective-permute-done | bytes 458784 | tf_op jit(solution)/shard_map/ppermute | solution.py:91
  56.7 5.5 %collective-permute-done.5 = bf16[128,1792]{1,0:T(8,128)(2,1)S(1)} collective-permute-done((bf16[128,1792]{1,0:T(8,128)(2,1)}, bf16[128,1792]{1,0:T(8,128)(2,1)S(1)}, u32[]{:S(2)}, u32[]{:S(2)}) %collective-permute-start.5) | collective-permute-done | bytes 458784 | tf_op jit(solution)/shard_map/ppermute | solution.py:91
  63.6 2.2 %fusion.34 = bf16[448,128]{1,0:T(8,128)(2,1)S(1)} fusion(bf16[128,3584]{1,0:T(8,128)(2,1)} %collective-permute-done.3, bf16[1,448,3584]{2,1,0:T(8,128)(2,1)S(1)} %copy-done), kind=kOutput, calls=%fused_computation.26 | convolution fusion | flops 411099136 | bytes 4243456 | tf_op jit(solution)/shard_map/dot_general | solution.py:82
  65.7 6.1 %collective-permute-done.9 = bf16[112,3584]{1,0:T(8,128)(2,1)S(1)} collective-permute-done((bf16[112,3584]{1,0:T(8,128)(2,1)}, bf16[112,3584]{1,0:T(8,128)(2,1)S(1)}, u32[]{:S(2)}, u32[]{:S(2)}) %collective-permute-start.9) | collective-permute-done | bytes 802848 | tf_op jit(solution)/shard_map/ppermute | solution.py:91
  72.0 2.2 %collective-permute-done.10 = bf16[112,3584]{1,0:T(8,128)(2,1)S(1)} collective-permute-done((bf16[112,3584]{1,0:T(8,128)(2,1)S(1)}, bf16[112,3584]{1,0:T(8,128)(2,1)S(1)}, u32[]{:S(2)}, u32[]{:S(2)}) %collective-permute-start.10) | collective-permute-done | bytes 802848 | tf_op jit(solution)/shard_map/ppermute | solution.py:91
  74.8 2.2 %convolution_convert_fusion.2 = bf16[448,128]{1,0:T(8,128)(2,1)S(1)} fusion(bf16[448,3584]{1,0:T(8,128)(2,1)S(1)} %constant_dynamic-update-slice_fusion, bf16[128,3584]{1,0:T(8,128)(2,1)} %collective-permute-done.3), kind=kOutput, calls=%fused_computation.24 | convolution fusion | flops 411099136 | bytes 4243456 | tf_op jit(solution)/shard_map/dot_general | solution.py:82
  77.6 1.3 %collective-permute-start.13 = (bf16[448,256]{1,0:T(8,128)(2,1)S(1)}, bf16[448,256]{1,0:T(8,128)(2,1)S(1)}, u32[]{:S(2)}, u32[]{:S(2)}) collective-permute-start(bf16[448,256]{1,0:T(8,128)(2,1)S(1)} %pad_maximum_fusion), channel_id=1, source_target_pairs={{1,0},{2,3},{5,4},{6,7},{9,8},{10,11},{13,12},{14,15},{17,16},{18,... | collective-permute-start | bytes 688136 | tf_op jit(solution)/shard_map/ppermute | solution.py:91
  81.2 1.0 %convolution_convert_fusion.1 = bf16[448,128]{1,0:T(8,128)(2,1)S(1)} fusion(bf16[448,3584]{1,0:T(8,128)(2,1)S(1)} %constant_dynamic-update-slice_fusion, bf16[128,3584]{1,0:T(8,128)(2,1)S(1)} %collective-permute-done.6), kind=kOutput, calls=%fused_computation.23 | convolution fusion | flops 411099136 | bytes 4243456 | tf_op jit(solution)/shard_map/dot_general | solution.py:82
  82.3 1.3 %collective-permute-start.12 = (bf16[448,128]{1,0:T(8,128)(2,1)S(1)}, bf16[448,128]{1,0:T(8,128)(2,1)S(1)}, u32[]{:S(2)}, u32[]{:S(2)}) collective-permute-start(bf16[448,128]{1,0:T(8,128)(2,1)S(1)} %add_convert_fusion), channel_id=1, source_target_pairs={{1,0},{2,3},{5,4},{6,7},{9,8},{10,11},{13,12},{14,15},{17,16},{18,... | collective-permute-start | bytes 344072 | tf_op jit(solution)/shard_map/ppermute | solution.py:91
  84.1 1.0 %fusion.35 = bf16[448,128]{1,0:T(8,128)(2,1)S(1)} fusion(bf16[128,3584]{1,0:T(8,128)(2,1)S(1)} %collective-permute-done.6, bf16[1,448,3584]{2,1,0:T(8,128)(2,1)S(1)} %copy-done), kind=kOutput, calls=%fused_computation.27 | convolution fusion | flops 411099136 | bytes 4243456 | tf_op jit(solution)/shard_map/dot_general | solution.py:82
  85.1 1.3 %collective-permute-start.14 = (bf16[448,128]{1,0:T(8,128)(2,1)S(1)}, bf16[448,128]{1,0:T(8,128)(2,1)S(1)}, u32[]{:S(2)}, u32[]{:S(2)}) collective-permute-start(bf16[448,128]{1,0:T(8,128)(2,1)S(1)} %convolution_convert_fusion.1), channel_id=1, source_target_pairs={{1,0},{2,3},{5,4},{6,7},{9,8},{10,11},{13,12},{14,15},{17,16},{18,... | collective-permute-start | bytes 344072 | tf_op jit(solution)/shard_map/ppermute | solution.py:91
  87.0 6.6 %collective-permute-done.14 = bf16[448,128]{1,0:T(8,128)(2,1)S(1)} collective-permute-done((bf16[448,128]{1,0:T(8,128)(2,1)S(1)}, bf16[448,128]{1,0:T(8,128)(2,1)S(1)}, u32[]{:S(2)}, u32[]{:S(2)}) %collective-permute-start.14) | collective-permute-done | bytes 114720 | tf_op jit(solution)/shard_map/ppermute | solution.py:91
  94.2 0.9 fusion.42
  (56 shorter events, 10.1 us)
Async XLA Ops:
  0.6 62.9 %copy-start = (bf16[1,448,3584]{2,1,0:T(8,128)(2,1)S(1)}, bf16[1,448,3584]{2,1,0:T(8,128)(2,1)}, u32[]{:S(2)}) copy-start(bf16[1,448,3584]{2,1,0:T(8,128)(2,1)} %param.9) | copy-start | bytes 9633796
  4.4 1.6 %collective-permute-start.15 = (f32[1,3584]{1,0:T(1,128)}, f32[1,3584]{1,0:T(1,128)S(1)}, u32[]{:S(2)}, u32[]{:S(2)}) collective-permute-start(f32[1,3584]{1,0:T(1,128)} %get-tuple-element.37), channel_id=1, source_target_pairs={{0,4},{4,0},{8,12},{12,8},{1,5},{5,1},{9,13},{13,9},{2,6},{6,2},{1... | collective-permute-start | bytes 43016 | tf_op jit(solution)/shard_map/ppermute | solution.py:91
  6.7 4.6 %collective-permute-start.16 = (f32[1,3584]{1,0:T(1,128)S(1)}, f32[1,3584]{1,0:T(1,128)S(1)}, u32[]{:S(2)}, u32[]{:S(2)}) collective-permute-start(f32[1,3584]{1,0:T(1,128)S(1)} %add.37), channel_id=1, source_target_pairs={{0,8},{4,12},{8,0},{12,4},{1,9},{5,13},{9,1},{13,5},{2,10},{6,14},... | collective-permute-start | bytes 43016 | tf_op jit(solution)/shard_map/ppermute | solution.py:91
  11.3 7.0 %collective-permute-start.17 = (f32[1,3584]{1,0:T(1,128)S(1)}, f32[1,3584]{1,0:T(1,128)S(1)}, u32[]{:S(2)}, u32[]{:S(2)}) collective-permute-start(f32[1,3584]{1,0:T(1,128)S(1)} %add.38), channel_id=1, source_target_pairs={{0,1},{3,2},{4,5},{7,6},{8,9},{11,10},{12,13},{15,14},{16,17},{19,... | collective-permute-start | bytes 43016 | tf_op jit(solution)/shard_map/ppermute | solution.py:91
  15.3 3.7 %collective-permute-start.18 = (f32[1,3584]{1,0:T(1,128)S(1)}, f32[1,3584]{1,0:T(1,128)S(1)}, u32[]{:S(2)}, u32[]{:S(2)}) collective-permute-start(f32[1,3584]{1,0:T(1,128)S(1)} %add.38), channel_id=1, source_target_pairs={{0,2},{3,1},{4,6},{7,5},{8,10},{11,9},{12,14},{15,13},{16,18},{19,... | collective-permute-start | bytes 43016 | tf_op jit(solution)/shard_map/ppermute | solution.py:91
  17.6 1.4 %collective-permute-start.19 = (f32[1,3584]{1,0:T(1,128)S(1)}, f32[1,3584]{1,0:T(1,128)S(1)}, u32[]{:S(2)}, u32[]{:S(2)}) collective-permute-start(f32[1,3584]{1,0:T(1,128)S(1)} %add.38), channel_id=1, source_target_pairs={{1,2},{2,1},{5,6},{6,5},{9,10},{10,9},{13,14},{14,13},{17,18},{18,... | collective-permute-start | bytes 43016 | tf_op jit(solution)/shard_map/ppermute | solution.py:91
  19.1 16.3 %collective-permute-start.20 = (f32[1,3584]{1,0:T(1,128)S(1)}, f32[1,3584]{1,0:T(1,128)S(1)}, u32[]{:S(2)}, u32[]{:S(2)}) collective-permute-start(f32[1,3584]{1,0:T(1,128)S(1)} %add_add_fusion), channel_id=1, source_target_pairs={{1,0},{2,3},{5,4},{6,7},{9,8},{10,11},{13,12},{14,15},{17,16},{18,... | collective-permute-start | bytes 43016 | tf_op jit(solution)/shard_map/ppermute | solution.py:91
  22.5 28.8 %collective-permute-start.7 = (bf16[112,3584]{1,0:T(8,128)(2,1)}, bf16[112,3584]{1,0:T(8,128)(2,1)}, u32[]{:S(2)}, u32[]{:S(2)}) collective-permute-start(bf16[112,3584]{1,0:T(8,128)(2,1)} %dynamic-slice_bitcast_fusion), channel_id=1, source_target_pairs={{0,1},{3,2},{4,5},{7,6},{8,9},{11,10},{12,13},{15,14},{16,17},{19,... | collective-permute-start | bytes 2408456 | tf_op jit(solution)/shard_map/ppermute | solution.py:91
  27.9 15.6 %collective-permute-start = (bf16[128,1792]{1,0:T(8,128)(2,1)}, bf16[128,1792]{1,0:T(8,128)(2,1)}, u32[]{:S(2)}, u32[]{:S(2)}) collective-permute-start(bf16[128,1792]{1,0:T(8,128)(2,1)} %get-tuple-element.27), channel_id=1, source_target_pairs={{16,0},{19,3},{0,16},{3,19},{20,4},{23,7},{4,20},{7,23},{24,8},{27... | collective-permute-start | bytes 1376264 | tf_op jit(solution)/shard_map/ppermute | solution.py:91
  31.3 18.7 %collective-permute-start.4 = (bf16[128,1792]{1,0:T(8,128)(2,1)}, bf16[128,1792]{1,0:T(8,128)(2,1)}, u32[]{:S(2)}, u32[]{:S(2)}) collective-permute-start(bf16[128,1792]{1,0:T(8,128)(2,1)} %get-tuple-element.28), channel_id=1, source_target_pairs={{16,0},{19,3},{0,16},{3,19},{20,4},{23,7},{4,20},{7,23},{24,8},{27... | collective-permute-start | bytes 1376264 | tf_op jit(solution)/shard_map/ppermute | solution.py:91
  33.7 29.1 %collective-permute-start.3 = (bf16[128,3584]{1,0:T(8,128)(2,1)}, bf16[128,3584]{1,0:T(8,128)(2,1)}, u32[]{:S(2)}, u32[]{:S(2)}) collective-permute-start(bf16[128,3584]{1,0:T(8,128)(2,1)} %get-tuple-element.26), channel_id=1, source_target_pairs={{17,2},{18,1},{1,18},{2,17},{21,6},{22,5},{5,22},{6,21},{25,10},{2... | collective-permute-start | bytes 2752520 | tf_op jit(solution)/shard_map/ppermute | solution.py:91
  43.5 12.5 %collective-permute-start.1 = (bf16[128,1792]{1,0:T(8,128)(2,1)}, bf16[128,1792]{1,0:T(8,128)(2,1)S(1)}, u32[]{:S(2)}, u32[]{:S(2)}) collective-permute-start(bf16[128,1792]{1,0:T(8,128)(2,1)} %collective-permute-done), channel_id=1, source_target_pairs={{0,1},{3,2},{4,5},{7,6},{8,9},{11,10},{12,13},{15,14},{16,17},{19,... | collective-permute-start | bytes 1376264 | tf_op jit(solution)/shard_map/ppermute | solution.py:91
  49.9 12.2 %collective-permute-start.5 = (bf16[128,1792]{1,0:T(8,128)(2,1)}, bf16[128,1792]{1,0:T(8,128)(2,1)S(1)}, u32[]{:S(2)}, u32[]{:S(2)}) collective-permute-start(bf16[128,1792]{1,0:T(8,128)(2,1)} %collective-permute-done.4), channel_id=1, source_target_pairs={{0,1},{3,2},{4,5},{7,6},{8,9},{11,10},{12,13},{15,14},{16,17},{19,... | collective-permute-start | bytes 1376264 | tf_op jit(solution)/shard_map/ppermute | solution.py:91
  51.3 20.6 %collective-permute-start.8 = (bf16[112,3584]{1,0:T(8,128)(2,1)}, bf16[112,3584]{1,0:T(8,128)(2,1)S(1)}, u32[]{:S(2)}, u32[]{:S(2)}) collective-permute-start(bf16[112,3584]{1,0:T(8,128)(2,1)} %collective-permute-done.7), channel_id=1, source_target_pairs={{0,4},{4,0},{8,12},{12,8},{1,5},{5,1},{9,13},{13,9},{2,6},{6,2},{1... | collective-permute-start | bytes 2408456 | tf_op jit(solution)/shard_map/ppermute | solution.py:91
  51.3 20.5 %collective-permute-start.9 = (bf16[112,3584]{1,0:T(8,128)(2,1)}, bf16[112,3584]{1,0:T(8,128)(2,1)S(1)}, u32[]{:S(2)}, u32[]{:S(2)}) collective-permute-start(bf16[112,3584]{1,0:T(8,128)(2,1)} %collective-permute-done.7), channel_id=1, source_target_pairs={{0,8},{4,12},{8,0},{12,4},{1,9},{5,13},{9,1},{13,5},{2,10},{6,14},... | collective-permute-start | bytes 2408456 | tf_op jit(solution)/shard_map/ppermute | solution.py:91
  56.0 22.9 %collective-permute-start.6 = (bf16[128,3584]{1,0:T(8,128)(2,1)}, bf16[128,3584]{1,0:T(8,128)(2,1)S(1)}, u32[]{:S(2)}, u32[]{:S(2)}) collective-permute-start(bf16[128,3584]{1,0:T(8,128)(2,1)} %get-tuple-element.26), channel_id=1, source_target_pairs={{17,1},{18,2},{1,17},{2,18},{21,5},{22,6},{5,21},{6,22},{25,9},{26... | collective-permute-start | bytes 2752520 | tf_op jit(solution)/shard_map/ppermute | solution.py:91
  62.2 17.3 %collective-permute-start.11 = (bf16[128,1792]{1,0:T(8,128)(2,1)S(1)}, bf16[128,1792]{1,0:T(8,128)(2,1)S(1)}, u32[]{:S(2)}, u32[]{:S(2)}) collective-permute-start(bf16[128,1792]{1,0:T(8,128)(2,1)S(1)} %collective-permute-done.5), channel_id=1, source_target_pairs={{1,2},{2,1},{5,6},{6,5},{9,10},{10,9},{13,14},{14,13},{17,18},{18,... | collective-permute-start | bytes 1376264 | tf_op jit(solution)/shard_map/ppermute | solution.py:91
  62.9 17.8 %collective-permute-start.2 = (bf16[128,1792]{1,0:T(8,128)(2,1)S(1)}, bf16[128,1792]{1,0:T(8,128)(2,1)S(1)}, u32[]{:S(2)}, u32[]{:S(2)}) collective-permute-start(bf16[128,1792]{1,0:T(8,128)(2,1)S(1)} %collective-permute-done.1), channel_id=1, source_target_pairs={{1,2},{2,1},{5,6},{6,5},{9,10},{10,9},{13,14},{14,13},{17,18},{18,... | collective-permute-start | bytes 1376264 | tf_op jit(solution)/shard_map/ppermute | solution.py:91
  71.9 2.3 %collective-permute-start.10 = (bf16[112,3584]{1,0:T(8,128)(2,1)S(1)}, bf16[112,3584]{1,0:T(8,128)(2,1)S(1)}, u32[]{:S(2)}, u32[]{:S(2)}) collective-permute-start(bf16[112,3584]{1,0:T(8,128)(2,1)S(1)} %collective-permute-done.9), channel_id=1, source_target_pairs={{0,4},{4,0},{8,12},{12,8},{1,5},{5,1},{9,13},{13,9},{2,6},{6,2},{1... | collective-permute-start | bytes 2408456 | tf_op jit(solution)/shard_map/ppermute | solution.py:91
  77.6 16.1 %collective-permute-start.13 = (bf16[448,256]{1,0:T(8,128)(2,1)S(1)}, bf16[448,256]{1,0:T(8,128)(2,1)S(1)}, u32[]{:S(2)}, u32[]{:S(2)}) collective-permute-start(bf16[448,256]{1,0:T(8,128)(2,1)S(1)} %pad_maximum_fusion), channel_id=1, source_target_pairs={{1,0},{2,3},{5,4},{6,7},{9,8},{10,11},{13,12},{14,15},{17,16},{18,... | collective-permute-start | bytes 688136 | tf_op jit(solution)/shard_map/ppermute | solution.py:91
  82.3 11.8 %collective-permute-start.12 = (bf16[448,128]{1,0:T(8,128)(2,1)S(1)}, bf16[448,128]{1,0:T(8,128)(2,1)S(1)}, u32[]{:S(2)}, u32[]{:S(2)}) collective-permute-start(bf16[448,128]{1,0:T(8,128)(2,1)S(1)} %add_convert_fusion), channel_id=1, source_target_pairs={{1,0},{2,3},{5,4},{6,7},{9,8},{10,11},{13,12},{14,15},{17,16},{18,... | collective-permute-start | bytes 344072 | tf_op jit(solution)/shard_map/ppermute | solution.py:91
  85.1 8.5 %collective-permute-start.14 = (bf16[448,128]{1,0:T(8,128)(2,1)S(1)}, bf16[448,128]{1,0:T(8,128)(2,1)S(1)}, u32[]{:S(2)}, u32[]{:S(2)}) collective-permute-start(bf16[448,128]{1,0:T(8,128)(2,1)S(1)} %convolution_convert_fusion.1), channel_id=1, source_target_pairs={{1,0},{2,3},{5,4},{6,7},{9,8},{10,11},{13,12},{14,15},{17,16},{18,... | collective-permute-start | bytes 344072 | tf_op jit(solution)/shard_map/ppermute | solution.py:91

commit v2 on v1

v2 whole, which is shorter than its diff:
```python
import functools
import math

import jax
import jax.numpy as jnp
from jax import lax
from jax.experimental import pallas as pl
from jax.experimental.pallas import tpu as pltpu
from jax.sharding import PartitionSpec as P

epsilon = 1e-05

CUTS = 1
CHUNKS = 3


def spans_of(dim, count):
    lanes = dim // 128
    edges = [128 * (lanes * at // count) for at in range(count)] + [dim]
    return [slice(a, b) for a, b in zip(edges, edges[1:])]


def norm_kernel(width, group, spans, x_ref, gain_ref, up_ref, res_ref, out_ref, *refs):
    chunk_refs, sum_ref, part_ref = refs[: len(spans)], refs[-2], refs[-1]
    rows, dim = x_ref.shape
    f32 = jnp.float32

    @pl.when(pl.program_id(0) == 0)
    def _():
        part_ref[...] = jnp.zeros_like(part_ref)

    @pl.loop(0, rows // group)
    def _(step):
        here = pl.ds(pl.multiple_of(step * group, group), group)
        squares = jnp.zeros((group, 128), f32)
        cross = jnp.zeros((group, 128), f32)
        for at in range(0, dim, width):
            cols = slice(at, at + width)
            v = x_ref[here, cols].astype(f32)
            s = up_ref[here, cols].astype(f32) * gain_ref[:, cols]
            vv, sv = v * v, s * v
            for lane in range(0, width, 128):
                squares += vv[:, lane : lane + 128]
                cross += sv[:, lane : lane + 128]
        inverse = lax.rsqrt(jnp.sum(squares, axis=-1, keepdims=True) / dim + epsilon)
        project = inverse * (jnp.sum(cross, axis=-1, keepdims=True) / dim)
        for at in range(0, dim, width):
            cols = slice(at, at + width)
            u = up_ref[here, cols].astype(f32)
            normed = x_ref[here, cols].astype(f32) * inverse
            moved = inverse * (u * gain_ref[:, cols] - normed * project)
            b = (res_ref[here, cols].astype(f32) + moved).astype(jnp.bfloat16)
            out_ref[here, cols] = b
            for span, ref in zip(spans, chunk_refs):
                if span.start <= at < span.stop:
                    ref[here, at - span.start : at - span.start + width] = b
            terms = u * normed
            part_ref[:, cols] += functools.reduce(jnp.add, [terms[at : at + 8] for at in range(0, group, 8)])

    @pl.when(pl.program_id(0) == pl.num_programs(0) - 1)
    def _():
        sum_ref[...] = jnp.sum(part_ref[...], axis=0, keepdims=True)


def norm_backward(x, gain, up, res, spans=()):
    rows, dim = x.shape
    block = math.gcd(rows, 64)
    width = functools.reduce(math.gcd, [s.start for s in spans], math.gcd(dim, 256))
    tile = lambda cols: pl.BlockSpec((block, cols), lambda i: (i, 0))
    row = pl.BlockSpec((1, dim), lambda i: (0, 0))
    shape = jax.ShapeDtypeStruct
    widths = [dim] + [s.stop - s.start for s in spans]
    results = pl.pallas_call(
        functools.partial(norm_kernel, width, math.gcd(block, 32), spans),
        grid=(rows // block,),
        in_specs=[tile(dim), row, tile(dim), tile(dim)],
        out_specs=[tile(w) for w in widths] + [row],
        out_shape=[shape((rows, w), jnp.bfloat16) for w in widths] + [shape((1, dim), jnp.float32)],
        scratch_shapes=[pltpu.VMEM((8, dim), jnp.float32)],
        cost_estimate=pl.CostEstimate(flops=12 * rows * dim, bytes_accessed=10 * rows * dim, transcendentals=rows),
        compiler_params=pltpu.CompilerParams(vmem_limit_bytes=61 * 2**20),
        name="norm_backward",
    )(x, gain, up, res)
    return results[0], results[1:-1], results[-1]


def dot(w, t):
    return lax.dot_general(w, t, (((1,), (1,)), ((), ())), preferred_element_type=jnp.float32)


def swap(axis, distance):
    count = lax.axis_size(axis)
    return [(at, at ^ distance) for at in range(count)]


def relay(norm_input, norm_gain, branch_grad, residual_grad, down_weight):
    weight = down_weight[0]
    hidden, dim = weight.shape
    copies = lax.axis_size("dp")
    me_dp, me = lax.axis_index("dp"), lax.axis_index("shard")
    last = lax.axis_size("shard") - 1
    flip = lambda at: last - at
    both = lambda route: route + [(flip(a), flip(b)) for a, b in route]
    inner, lower = (me != 0) & (me != last), me <= last // 2
    flags = [inner, lower] + [(me_dp & 1 << bit) != 0 for bit in range(copies.bit_length() - 1)]
    norm_input, (inner, lower, *crossed) = lax.optimization_barrier((norm_input, flags))
    inward, across, outward = both([(0, 1)]), both([(1, 2)]), both([(1, 0)])
    count = last + 1
    cross = lambda route: [((1 - g) * count + a, g * count + b) for g in (0, 1) for a, b in route]
    other = ("section", "shard")

    part = hidden // copies
    slab = part // CUTS
    spans = spans_of(dim, CHUNKS)
    bf16 = jnp.bfloat16

    pieces = []
    for cut in range(CUTS):
        piece = lax.dynamic_slice_in_dim(weight, me_dp * part + cut * slab, slab, axis=0)
        pieces.append((0, cut, lax.ppermute(piece, "shard", inward)))
    boundary, chunks, gain = norm_backward(
        norm_input[0, 0], norm_gain, branch_grad[0, 0], residual_grad[0, 0], spans
    )
    rows = boundary.shape[0]

    ends = cross(both([(0, 0)]))
    far = lax.ppermute(boundary, other, cross(across))
    near = lax.ppermute(boundary, other, cross(both([(1, 1)])))
    outer = [lax.ppermute(chunk, other, ends) for chunk in chunks]
    rim = [lax.ppermute(chunk, "shard", inward) for chunk in outer]
    tail = [lax.ppermute(chunk, "shard", across) for chunk in rim]

    distance = 1
    while distance < copies:
        gain = gain + lax.ppermute(gain, "dp", swap("dp", distance))
        distance *= 2
    for route in (inward, across):
        moved = lax.ppermute(gain, "shard", route)
        gain = gain + moved
    gain_out = lax.ppermute(gain, "shard", outward)

    distance = copies // 2
    while distance:
        pieces += [
            (at ^ distance, cut, lax.ppermute(block, "dp", swap("dp", distance)))
            for at, cut, block in list(pieces)
        ]
        distance //= 2
    edge_weight = jnp.concatenate([block for _, _, block in sorted(pieces, key=lambda t: t[:2])])

    def whole(w, t):
        return [dot(w, t)]

    def parts(w, blocks):
        return [dot(w[:, s], block) for s, block in zip(spans, blocks)]

    def total(terms):
        return functools.reduce(jnp.add, terms).astype(bf16)

    own, edge = {}, {}
    edge["far"] = total(whole(edge_weight, far))
    local = total(parts(weight, outer))
    one = lax.ppermute(edge["far"], "shard", outward)
    near, edge["far"] = lax.optimization_barrier((near, edge["far"]))
    edge["near"] = dot(edge_weight, near).astype(bf16)
    two = lax.ppermute(edge["near"], "shard", outward)
    begun = parts(edge_weight, tail[:-1])
    tail[-1], begun = lax.optimization_barrier((tail[-1], begun))
    edge["tail"] = total(begun + [dot(edge_weight[:, spans[-1]], tail[-1])])
    three = lax.ppermute(edge["tail"], "shard", outward)
    far, rim, near, tail, _ = lax.optimization_barrier((far, rim, near, tail, edge["tail"]))
    own["far"] = total(whole(weight, far))
    own["edge"] = total(parts(weight, rim))
    own["near"] = dot(weight, near).astype(bf16)
    own["tail"] = total(parts(weight, tail))
    one, two, own, local = lax.optimization_barrier((one, two, own, local))
    gain_grad = jnp.where(inner, gain, gain_out) / (rows * count)

    def restore(block):
        block = block.reshape(copies, part, rows)
        for bit, flip in enumerate(crossed):
            moved = jnp.stack([block[at ^ 1 << bit] for at in range(copies)])
            block = jnp.where(flip, moved, block)
        return block.reshape(hidden, rows)

    got = {"far": restore(one), "near": restore(two), "edge": local}
    result = {name: jnp.where(inner, own[name], got[name]) for name in got}
    names = tuple(result)
    ready = lax.optimization_barrier((three, own["tail"], gain_grad) + tuple(result[name] for name in names))
    three, own["tail"], gain_grad = ready[:3]
    result = dict(zip(names, ready[3:]))
    result["tail"] = jnp.where(inner, own["tail"], restore(three))
    up = jnp.concatenate([result[name] for name in ("edge", "near", "far", "tail")], axis=1)
    down = jnp.concatenate([result[name] for name in ("tail", "far", "near", "edge")], axis=1)
    fresh = jnp.where(lower, up, down).T
    return (boundary[None, None], gain_grad, fresh[None, None])


def gather(norm_input, norm_gain, branch_grad, residual_grad, down_weight):
    boundary, _, gain = norm_backward(norm_input[0, 0], norm_gain, branch_grad[0, 0], residual_grad[0, 0])
    arrived = lax.ppermute(boundary, "section", swap("section", 1))
    fresh = jnp.einsum(
        "nd,hd->nh",
        lax.all_gather(arrived, "shard", axis=0, tiled=True),
        down_weight[0],
        preferred_element_type=jnp.float32,
    ).astype(jnp.bfloat16)
    gain_grad = lax.psum(gain, ("dp", "shard")) / fresh.shape[0]
    return (boundary[None, None], gain_grad, fresh[None, None])


def solution(mesh):
    in_specs = (
        P("section", "dp", "shard", None),
        P("section", None),
        P("section", "dp", "shard", None),
        P("section", "dp", "shard", None),
        P("section", "shard", None),
    )
    out_specs = (
        P("section", "dp", "shard", None),
        P("section", None),
        P("section", "dp", None, "shard"),
    )
    line = mesh.shape["shard"] == 4 and mesh.shape["section"] == 2
    mapped = functools.partial(jax.shard_map, mesh=mesh, in_specs=in_specs, out_specs=out_specs, check_vma=False)
    if not line:
        return mapped(gather)
    return mapped(relay)
```

time: 95.8 us -> 113 us (1.18)
  waiting for transfers between devices: 38.4 us -> 51.7 us
  starting transfers between devices: 34.8 us -> 41.2 us
  local copies, waits for them, and re-layouts: 3.6 us -> 1.49 us
    ppermute x21 -> x23, waiting for transfers between devices: 38.4 us -> 51.7 us  [the longest x1 26.2 us: relay(): two = lax.ppermute(edge['near'], 'shard', outward)]
    ppermute x21 -> x23, starting transfers between devices: 34.8 us -> 41.2 us  [the longest x3 9.24 us: relay(): outer = [lax.ppermute(chunk, other, ends) for chunk in chunks]]
    unnamed x5 -> x7, local copies, waits for them, and re-layouts: 1.34 us -> 0.17 us
    dot_general x12 -> x16, matrix products: 10.9 us -> 10.4 us  [dot(): lax.dot_general(w, t, (((1,), (1,)), ((), ())), preferred_element_type=jn...]
  transfers between devices with their start and end apart: 21 -> 23, of which waited for: 10 -> 8; matrix products, arithmetic and copies ran while one was open for 16% -> 11% of each run, Pallas kernels for 0% -> 0%
where the time goes in v2:
time: 113 us; the launch traced here: 112 us
  waiting for transfers between devices  51.7 us (46%)
  starting transfers between devices  41.2 us (36%)
  matrix products  10.4 us (9%)
  Pallas kernels  3.7 us (3%)
  other arithmetic  2.58 us (2%)
  local copies, waits for them, and re-layouts  1.49 us (1%)
  between operations  1.19 us (1%)
    ppermute x1, waiting for transfers between devices, relay(): two = lax.ppermute(edge['near'], 'shard', outward)  26.2 us
    ppermute x3, waiting for transfers between devices, relay(): lax.ppermute(block, 'dp', swap('dp', distance))  15.5 us
    dot_general x16, matrix products, dot(): lax.dot_general(w, t, (((1,), (1,)), ((), ())), preferred_element_type=jn...  10.4 us
    ppermute x3, starting transfers between devices, relay(): outer = [lax.ppermute(chunk, other, ends) for chunk in chunks]  9.24 us
    ppermute x1, starting transfers between devices, relay(): pieces.append((0, cut, lax.ppermute(piece, 'shard', inward)))  9.17 us
    ppermute x3, waiting for transfers between devices, relay(): outer = [lax.ppermute(chunk, other, ends) for chunk in chunks]  5.81 us
    ppermute x2, starting transfers between devices, relay(): moved = lax.ppermute(gain, 'shard', route)  4.64 us
    ppermute x3, starting transfers between devices, relay(): rim = [lax.ppermute(chunk, 'shard', inward) for chunk in outer]  4.43 us
  transfers between devices with their start and end apart: 23, of which 8 were waited for; matrix products, arithmetic and copies ran while one was open for 11% of the time, Pallas kernels for 0%

profile of v2, /device:TPU:0, one launch (start us, length us, event | category | flops | bytes accessed | tf_op | source)
XLA Modules:
  0.0 112.3 jit_solution(12626950781565086301)
XLA Ops:
  0.6 3.7 %norm_backward.1 = (bf16[128,3584]{1,0:T(8,128)(2,1)}, bf16[128,1152]{1,0:T(8,128)(2,1)}, bf16[128,1152]{1,0:T(8,128)(2,1)}, bf16[128,1280]{1,0:T(8,128)(2,1)}, f32[1,3584]{1,0:T(1,128)}) custom-call(bf16[128,3584]{1,0:T(8,128)(2,1)} %bitcast.106, f32[1,3584]{1,0:T(1,128)} %gain_ref.1, bf16[128,3584]{1,0:T(8,128)(2,1)} %bitcast.107, bf16[128,3584]{1,0:T(8,128)(2,1)} %bitcast.108), custom_call_target="tpu_custom_call" | custom-call | flops 5505024 | bytes 4587520 | tf_op jit(solution)/shard_map/norm_backward/pallas_call | solution.py:73
  4.9 1.0 collective-permute-done.18
  6.0 0.7 add.54
  6.7 2.9 %collective-permute-start.19 = (f32[1,3584]{1,0:T(1,128)S(1)}, f32[1,3584]{1,0:T(1,128)S(1)}, u32[]{:S(2)}, u32[]{:S(2)}) collective-permute-start(f32[1,3584]{1,0:T(1,128)S(1)} %add.54), channel_id=1, source_target_pairs={{0,8},{4,12},{8,0},{12,4},{1,9},{5,13},{9,1},{13,5},{2,10},{6,14},... | collective-permute-start | bytes 43016 | tf_op jit(solution)/shard_map/ppermute | solution.py:135
  9.6 1.7 %collective-permute-done.19 = f32[1,3584]{1,0:T(1,128)S(1)} collective-permute-done((f32[1,3584]{1,0:T(1,128)S(1)}, f32[1,3584]{1,0:T(1,128)S(1)}, u32[]{:S(2)}, u32[]{:S(2)}) %collective-permute-start.19) | collective-permute-done | bytes 14368 | tf_op jit(solution)/shard_map/ppermute | solution.py:135
  11.3 4.0 %collective-permute-start.20 = (f32[1,3584]{1,0:T(1,128)S(1)}, f32[1,3584]{1,0:T(1,128)S(1)}, u32[]{:S(2)}, u32[]{:S(2)}) collective-permute-start(f32[1,3584]{1,0:T(1,128)S(1)} %add.55), channel_id=1, source_target_pairs={{0,1},{3,2},{4,5},{7,6},{8,9},{11,10},{12,13},{15,14},{16,17},{19,... | collective-permute-start | bytes 43016 | tf_op jit(solution)/shard_map/ppermute | solution.py:138
  15.3 1.4 %collective-permute-done.20 = f32[1,3584]{1,0:T(1,128)S(1)} collective-permute-done((f32[1,3584]{1,0:T(1,128)S(1)}, f32[1,3584]{1,0:T(1,128)S(1)}, u32[]{:S(2)}, u32[]{:S(2)}) %collective-permute-start.20) | collective-permute-done | bytes 14368 | tf_op jit(solution)/shard_map/ppermute | solution.py:138
  17.4 1.3 %collective-permute-start.22 = (f32[1,3584]{1,0:T(1,128)S(1)}, f32[1,3584]{1,0:T(1,128)S(1)}, u32[]{:S(2)}, u32[]{:S(2)}) collective-permute-start(f32[1,3584]{1,0:T(1,128)S(1)} %add.57), channel_id=1, source_target_pairs={{1,0},{2,3},{5,4},{6,7},{9,8},{10,11},{13,12},{14,15},{17,16},{18,... | collective-permute-start | bytes 43016 | tf_op jit(solution)/shard_map/ppermute | solution.py:140
  18.7 1.2 %dynamic-slice_bitcast_fusion = bf16[112,3584]{1,0:T(8,128)(2,1)S(1)} fusion(bf16[1,448,3584]{2,1,0:T(8,128)(2,1)} %param.9, s32[]{:T(128)S(6)} %select_n.83), kind=kLoop, calls=%fused_computation.30 | loop fusion | bytes 1605636 | tf_op jit(solution)/shard_map/dynamic_slice | solution.py:119
  20.0 9.2 %collective-permute-start.3 = (bf16[112,3584]{1,0:T(8,128)(2,1)S(1)}, bf16[112,3584]{1,0:T(8,128)(2,1)S(1)}, u32[]{:S(2)}, u32[]{:S(2)}) collective-permute-start(bf16[112,3584]{1,0:T(8,128)(2,1)S(1)} %dynamic-slice_bitcast_fusion), channel_id=1, source_target_pairs={{0,1},{3,2},{4,5},{7,6},{8,9},{11,10},{12,13},{15,14},{16,17},{19,... | collective-permute-start | bytes 2408456 | tf_op jit(solution)/shard_map/ppermute | solution.py:120
  29.1 3.4 %collective-permute-start.10 = (bf16[128,1152]{1,0:T(8,128)(2,1)}, bf16[128,1152]{1,0:T(8,128)(2,1)S(1)}, u32[]{:S(2)}, u32[]{:S(2)}) collective-permute-start(bf16[128,1152]{1,0:T(8,128)(2,1)} %get-tuple-element.42), channel_id=1, source_target_pairs={{16,0},{19,3},{0,16},{3,19},{20,4},{23,7},{4,20},{7,23},{24,8},{27... | collective-permute-start | bytes 884744 | tf_op jit(solution)/shard_map/ppermute | solution.py:129
  32.5 2.4 %collective-permute-start.7 = (bf16[128,1152]{1,0:T(8,128)(2,1)}, bf16[128,1152]{1,0:T(8,128)(2,1)S(1)}, u32[]{:S(2)}, u32[]{:S(2)}) collective-permute-start(bf16[128,1152]{1,0:T(8,128)(2,1)} %get-tuple-element.41), channel_id=1, source_target_pairs={{16,0},{19,3},{0,16},{3,19},{20,4},{23,7},{4,20},{7,23},{24,8},{27... | collective-permute-start | bytes 884744 | tf_op jit(solution)/shard_map/ppermute | solution.py:129
  35.0 3.4 %collective-permute-start = (bf16[128,1280]{1,0:T(8,128)(2,1)}, bf16[128,1280]{1,0:T(8,128)(2,1)S(1)}, u32[]{:S(2)}, u32[]{:S(2)}) collective-permute-start(bf16[128,1280]{1,0:T(8,128)(2,1)} %get-tuple-element.40), channel_id=1, source_target_pairs={{16,0},{19,3},{0,16},{3,19},{20,4},{23,7},{4,20},{7,23},{24,8},{27... | collective-permute-start | bytes 983048 | tf_op jit(solution)/shard_map/ppermute | solution.py:129
  38.4 0.7 collective-permute-start.14
  39.8 1.4 %collective-permute-done.10 = bf16[128,1152]{1,0:T(8,128)(2,1)S(1)} collective-permute-done((bf16[128,1152]{1,0:T(8,128)(2,1)}, bf16[128,1152]{1,0:T(8,128)(2,1)S(1)}, u32[]{:S(2)}, u32[]{:S(2)}) %collective-permute-start.10) | collective-permute-done | bytes 294944 | tf_op jit(solution)/shard_map/ppermute | solution.py:129
  41.1 1.3 %collective-permute-start.11 = (bf16[128,1152]{1,0:T(8,128)(2,1)S(1)}, bf16[128,1152]{1,0:T(8,128)(2,1)S(1)}, u32[]{:S(2)}, u32[]{:S(2)}) collective-permute-start(bf16[128,1152]{1,0:T(8,128)(2,1)S(1)} %collective-permute-done.10), channel_id=1, source_target_pairs={{0,1},{3,2},{4,5},{7,6},{8,9},{11,10},{12,13},{15,14},{16,17},{19,... | collective-permute-start | bytes 884744 | tf_op jit(solution)/shard_map/ppermute | solution.py:130
  42.4 4.0 %collective-permute-done.7 = bf16[128,1152]{1,0:T(8,128)(2,1)S(1)} collective-permute-done((bf16[128,1152]{1,0:T(8,128)(2,1)}, bf16[128,1152]{1,0:T(8,128)(2,1)S(1)}, u32[]{:S(2)}, u32[]{:S(2)}) %collective-permute-start.7) | collective-permute-done | bytes 294944 | tf_op jit(solution)/shard_map/ppermute | solution.py:129
  46.4 1.3 %collective-permute-start.8 = (bf16[128,1152]{1,0:T(8,128)(2,1)S(1)}, bf16[128,1152]{1,0:T(8,128)(2,1)S(1)}, u32[]{:S(2)}, u32[]{:S(2)}) collective-permute-start(bf16[128,1152]{1,0:T(8,128)(2,1)S(1)} %collective-permute-done.7), channel_id=1, source_target_pairs={{0,1},{3,2},{4,5},{7,6},{8,9},{11,10},{12,13},{15,14},{16,17},{19,... | collective-permute-start | bytes 884744 | tf_op jit(solution)/shard_map/ppermute | solution.py:130
  47.7 1.7 %fusion.23 = f32[128,448]{0,1:T(8,128)S(1)} fusion(bf16[128,1152]{1,0:T(8,128)(2,1)S(1)} %collective-permute-done.10, bf16[448,3584]{1,0:T(8,128)(2,1)} %bitcast.94), kind=kOutput, calls=%fused_computation.31 | convolution fusion | flops 132120576 | bytes 1556480 | tf_op jit(solution)/shard_map/dot_general | solution.py:88
  49.9 1.5 %collective-permute-start.5 = (bf16[112,3584]{1,0:T(8,128)(2,1)S(1)}, bf16[112,3584]{1,0:T(8,128)(2,1)S(1)}, u32[]{:S(2)}, u32[]{:S(2)}) collective-permute-start(bf16[112,3584]{1,0:T(8,128)(2,1)S(1)} %collective-permute-done.3), channel_id=1, source_target_pairs={{0,8},{4,12},{8,0},{12,4},{1,9},{5,13},{9,1},{13,5},{2,10},{6,14},... | collective-permute-start | bytes 2408456 | tf_op jit(solution)/shard_map/ppermute | solution.py:145
  52.4 1.8 %collective-permute-start.1 = (bf16[128,1280]{1,0:T(8,128)(2,1)S(1)}, bf16[128,1280]{1,0:T(8,128)(2,1)S(1)}, u32[]{:S(2)}, u32[]{:S(2)}) collective-permute-start(bf16[128,1280]{1,0:T(8,128)(2,1)S(1)} %collective-permute-done), channel_id=1, source_target_pairs={{0,1},{3,2},{4,5},{7,6},{8,9},{11,10},{12,13},{15,14},{16,17},{19,... | collective-permute-start | bytes 983048 | tf_op jit(solution)/shard_map/ppermute | solution.py:130
  54.3 15.5 %collective-permute-done.5 = bf16[112,3584]{1,0:T(8,128)(2,1)S(1)} collective-permute-done((bf16[112,3584]{1,0:T(8,128)(2,1)S(1)}, bf16[112,3584]{1,0:T(8,128)(2,1)S(1)}, u32[]{:S(2)}, u32[]{:S(2)}) %collective-permute-start.5) | collective-permute-done | bytes 802848 | tf_op jit(solution)/shard_map/ppermute | solution.py:145
  69.9 0.7 collective-permute-start.16
  73.7 1.0 convolution_convert_fusion.3
  74.7 1.3 %collective-permute-start.15 = (bf16[448,128]{1,0:T(8,128)(2,1)S(1)}, bf16[448,128]{1,0:T(8,128)(2,1)S(1)}, u32[]{:S(2)}, u32[]{:S(2)}) collective-permute-start(bf16[448,128]{1,0:T(8,128)(2,1)S(1)} %convolution_convert_fusion.3), channel_id=1, source_target_pairs={{1,0},{2,3},{5,4},{6,7},{9,8},{10,11},{13,12},{14,15},{17,16},{18,... | collective-permute-start | bytes 344072 | tf_op jit(solution)/shard_map/ppermute | solution.py:163
  76.0 1.0 convolution_convert_fusion.2
  77.5 1.3 %collective-permute-start.13 = (bf16[448,128]{1,0:T(8,128)(2,1)S(1)}, bf16[448,128]{1,0:T(8,128)(2,1)S(1)}, u32[]{:S(2)}, u32[]{:S(2)}) collective-permute-start(bf16[448,128]{1,0:T(8,128)(2,1)S(1)} %add_convert_fusion), channel_id=1, source_target_pairs={{1,0},{2,3},{5,4},{6,7},{9,8},{10,11},{13,12},{14,15},{17,16},{18,... | collective-permute-start | bytes 344072 | tf_op jit(solution)/shard_map/ppermute | solution.py:170
  80.6 1.0 fusion.8
  81.6 1.0 fusion.9
  82.6 1.3 %collective-permute-start.17 = (bf16[448,128]{1,0:T(8,128)(2,1)S(1)}, bf16[448,128]{1,0:T(8,128)(2,1)S(1)}, u32[]{:S(2)}, u32[]{:S(2)}) collective-permute-start(bf16[448,128]{1,0:T(8,128)(2,1)S(1)} %convolution_convert_fusion.2), channel_id=1, source_target_pairs={{1,0},{2,3},{5,4},{6,7},{9,8},{10,11},{13,12},{14,15},{17,16},{18,... | collective-permute-start | bytes 344072 | tf_op jit(solution)/shard_map/ppermute | solution.py:166
  84.8 26.2 %collective-permute-done.17 = bf16[448,128]{1,0:T(8,128)(2,1)S(1)} collective-permute-done((bf16[448,128]{1,0:T(8,128)(2,1)S(1)}, bf16[448,128]{1,0:T(8,128)(2,1)S(1)}, u32[]{:S(2)}, u32[]{:S(2)}) %collective-permute-start.17) | collective-permute-done | bytes 114720 | tf_op jit(solution)/shard_map/ppermute | solution.py:166
  111.4 0.9 fusion.32
  (61 shorter events, 9.9 us)
Async XLA Ops:
  4.3 47.1 %copy-start = (bf16[1,448,3584]{2,1,0:T(8,128)(2,1)S(1)}, bf16[1,448,3584]{2,1,0:T(8,128)(2,1)}, u32[]{:S(2)}) copy-start(bf16[1,448,3584]{2,1,0:T(8,128)(2,1)} %param.9) | copy-start | bytes 9633796
  4.4 1.6 %collective-permute-start.18 = (f32[1,3584]{1,0:T(1,128)}, f32[1,3584]{1,0:T(1,128)S(1)}, u32[]{:S(2)}, u32[]{:S(2)}) collective-permute-start(f32[1,3584]{1,0:T(1,128)} %get-tuple-element.57), channel_id=1, source_target_pairs={{0,4},{4,0},{8,12},{12,8},{1,5},{5,1},{9,13},{13,9},{2,6},{6,2},{1... | collective-permute-start | bytes 43016 | tf_op jit(solution)/shard_map/ppermute | solution.py:135
  6.7 4.6 %collective-permute-start.19 = (f32[1,3584]{1,0:T(1,128)S(1)}, f32[1,3584]{1,0:T(1,128)S(1)}, u32[]{:S(2)}, u32[]{:S(2)}) collective-permute-start(f32[1,3584]{1,0:T(1,128)S(1)} %add.54), channel_id=1, source_target_pairs={{0,8},{4,12},{8,0},{12,4},{1,9},{5,13},{9,1},{13,5},{2,10},{6,14},... | collective-permute-start | bytes 43016 | tf_op jit(solution)/shard_map/ppermute | solution.py:135
  11.3 5.4 %collective-permute-start.20 = (f32[1,3584]{1,0:T(1,128)S(1)}, f32[1,3584]{1,0:T(1,128)S(1)}, u32[]{:S(2)}, u32[]{:S(2)}) collective-permute-start(f32[1,3584]{1,0:T(1,128)S(1)} %add.55), channel_id=1, source_target_pairs={{0,1},{3,2},{4,5},{7,6},{8,9},{11,10},{12,13},{15,14},{16,17},{19,... | collective-permute-start | bytes 43016 | tf_op jit(solution)/shard_map/ppermute | solution.py:138
  16.7 0.7 collective-permute-start.21
  17.4 20.9 %collective-permute-start.22 = (f32[1,3584]{1,0:T(1,128)S(1)}, f32[1,3584]{1,0:T(1,128)S(1)}, u32[]{:S(2)}, u32[]{:S(2)}) collective-permute-start(f32[1,3584]{1,0:T(1,128)S(1)} %add.57), channel_id=1, source_target_pairs={{1,0},{2,3},{5,4},{6,7},{9,8},{10,11},{13,12},{14,15},{17,16},{18,... | collective-permute-start | bytes 43016 | tf_op jit(solution)/shard_map/ppermute | solution.py:140
  20.0 29.4 %collective-permute-start.3 = (bf16[112,3584]{1,0:T(8,128)(2,1)S(1)}, bf16[112,3584]{1,0:T(8,128)(2,1)S(1)}, u32[]{:S(2)}, u32[]{:S(2)}) collective-permute-start(bf16[112,3584]{1,0:T(8,128)(2,1)S(1)} %dynamic-slice_bitcast_fusion), channel_id=1, source_target_pairs={{0,1},{3,2},{4,5},{7,6},{8,9},{11,10},{12,13},{15,14},{16,17},{19,... | collective-permute-start | bytes 2408456 | tf_op jit(solution)/shard_map/ppermute | solution.py:120
  29.1 12.0 %collective-permute-start.10 = (bf16[128,1152]{1,0:T(8,128)(2,1)}, bf16[128,1152]{1,0:T(8,128)(2,1)S(1)}, u32[]{:S(2)}, u32[]{:S(2)}) collective-permute-start(bf16[128,1152]{1,0:T(8,128)(2,1)} %get-tuple-element.42), channel_id=1, source_target_pairs={{16,0},{19,3},{0,16},{3,19},{20,4},{23,7},{4,20},{7,23},{24,8},{27... | collective-permute-start | bytes 884744 | tf_op jit(solution)/shard_map/ppermute | solution.py:129
  32.5 13.9 %collective-permute-start.7 = (bf16[128,1152]{1,0:T(8,128)(2,1)}, bf16[128,1152]{1,0:T(8,128)(2,1)S(1)}, u32[]{:S(2)}, u32[]{:S(2)}) collective-permute-start(bf16[128,1152]{1,0:T(8,128)(2,1)} %get-tuple-element.41), channel_id=1, source_target_pairs={{16,0},{19,3},{0,16},{3,19},{20,4},{23,7},{4,20},{7,23},{24,8},{27... | collective-permute-start | bytes 884744 | tf_op jit(solution)/shard_map/ppermute | solution.py:129
  35.0 14.9 %collective-permute-start = (bf16[128,1280]{1,0:T(8,128)(2,1)}, bf16[128,1280]{1,0:T(8,128)(2,1)S(1)}, u32[]{:S(2)}, u32[]{:S(2)}) collective-permute-start(bf16[128,1280]{1,0:T(8,128)(2,1)} %get-tuple-element.40), channel_id=1, source_target_pairs={{16,0},{19,3},{0,16},{3,19},{20,4},{23,7},{4,20},{7,23},{24,8},{27... | collective-permute-start | bytes 983048 | tf_op jit(solution)/shard_map/ppermute | solution.py:129
  38.4 35.3 %collective-permute-start.14 = (bf16[128,3584]{1,0:T(8,128)(2,1)}, bf16[128,3584]{1,0:T(8,128)(2,1)S(1)}, u32[]{:S(2)}, u32[]{:S(2)}) collective-permute-start(bf16[128,3584]{1,0:T(8,128)(2,1)} %get-tuple-element.39), channel_id=1, source_target_pairs={{17,2},{18,1},{1,18},{2,17},{21,6},{22,5},{5,22},{6,21},{25,10},{2... | collective-permute-start | bytes 2752520 | tf_op jit(solution)/shard_map/ppermute | solution.py:127
  41.1 28.8 %collective-permute-start.11 = (bf16[128,1152]{1,0:T(8,128)(2,1)S(1)}, bf16[128,1152]{1,0:T(8,128)(2,1)S(1)}, u32[]{:S(2)}, u32[]{:S(2)}) collective-permute-start(bf16[128,1152]{1,0:T(8,128)(2,1)S(1)} %collective-permute-done.10), channel_id=1, source_target_pairs={{0,1},{3,2},{4,5},{7,6},{8,9},{11,10},{12,13},{15,14},{16,17},{19,... | collective-permute-start | bytes 884744 | tf_op jit(solution)/shard_map/ppermute | solution.py:130
  46.4 24.2 %collective-permute-start.8 = (bf16[128,1152]{1,0:T(8,128)(2,1)S(1)}, bf16[128,1152]{1,0:T(8,128)(2,1)S(1)}, u32[]{:S(2)}, u32[]{:S(2)}) collective-permute-start(bf16[128,1152]{1,0:T(8,128)(2,1)S(1)} %collective-permute-done.7), channel_id=1, source_target_pairs={{0,1},{3,2},{4,5},{7,6},{8,9},{11,10},{12,13},{15,14},{16,17},{19,... | collective-permute-start | bytes 884744 | tf_op jit(solution)/shard_map/ppermute | solution.py:130
  49.4 3.0 %collective-permute-start.4 = (bf16[112,3584]{1,0:T(8,128)(2,1)S(1)}, bf16[112,3584]{1,0:T(8,128)(2,1)S(1)}, u32[]{:S(2)}, u32[]{:S(2)}) collective-permute-start(bf16[112,3584]{1,0:T(8,128)(2,1)S(1)} %collective-permute-done.3), channel_id=1, source_target_pairs={{0,4},{4,0},{8,12},{12,8},{1,5},{5,1},{9,13},{13,9},{2,6},{6,2},{1... | collective-permute-start | bytes 2408456 | tf_op jit(solution)/shard_map/ppermute | solution.py:145
  49.9 19.8 %collective-permute-start.5 = (bf16[112,3584]{1,0:T(8,128)(2,1)S(1)}, bf16[112,3584]{1,0:T(8,128)(2,1)S(1)}, u32[]{:S(2)}, u32[]{:S(2)}) collective-permute-start(bf16[112,3584]{1,0:T(8,128)(2,1)S(1)} %collective-permute-done.3), channel_id=1, source_target_pairs={{0,8},{4,12},{8,0},{12,4},{1,9},{5,13},{9,1},{13,5},{2,10},{6,14},... | collective-permute-start | bytes 2408456 | tf_op jit(solution)/shard_map/ppermute | solution.py:145
  51.9 18.0 %copy-start.1 = (bf16[128,3584]{1,0:T(8,128)(2,1)S(1)}, bf16[128,3584]{1,0:T(8,128)(2,1)}, u32[]{:S(2)}) copy-start(bf16[128,3584]{1,0:T(8,128)(2,1)} %get-tuple-element.39) | copy-start | bytes 2752516
  52.4 18.9 %collective-permute-start.1 = (bf16[128,1280]{1,0:T(8,128)(2,1)S(1)}, bf16[128,1280]{1,0:T(8,128)(2,1)S(1)}, u32[]{:S(2)}, u32[]{:S(2)}) collective-permute-start(bf16[128,1280]{1,0:T(8,128)(2,1)S(1)} %collective-permute-done), channel_id=1, source_target_pairs={{0,1},{3,2},{4,5},{7,6},{8,9},{11,10},{12,13},{15,14},{16,17},{19,... | collective-permute-start | bytes 983048 | tf_op jit(solution)/shard_map/ppermute | solution.py:130
  69.8 2.3 %collective-permute-start.6 = (bf16[112,3584]{1,0:T(8,128)(2,1)S(1)}, bf16[112,3584]{1,0:T(8,128)(2,1)S(1)}, u32[]{:S(2)}, u32[]{:S(2)}) collective-permute-start(bf16[112,3584]{1,0:T(8,128)(2,1)S(1)} %collective-permute-done.5), channel_id=1, source_target_pairs={{0,4},{4,0},{8,12},{12,8},{1,5},{5,1},{9,13},{13,9},{2,6},{6,2},{1... | collective-permute-start | bytes 2408456 | tf_op jit(solution)/shard_map/ppermute | solution.py:145
  69.9 6.1 %collective-permute-start.16 = (bf16[128,3584]{1,0:T(8,128)(2,1)S(1)}, bf16[128,3584]{1,0:T(8,128)(2,1)S(1)}, u32[]{:S(2)}, u32[]{:S(2)}) collective-permute-start(bf16[128,3584]{1,0:T(8,128)(2,1)S(1)} %copy-done.1), channel_id=1, source_target_pairs={{17,1},{18,2},{1,17},{2,18},{21,5},{22,6},{5,21},{6,22},{25,9},{26... | collective-permute-start | bytes 2752520 | tf_op jit(solution)/shard_map/ppermute | solution.py:128
  70.6 2.2 %collective-permute-start.12 = (bf16[128,1152]{1,0:T(8,128)(2,1)S(1)}, bf16[128,1152]{1,0:T(8,128)(2,1)S(1)}, u32[]{:S(2)}, u32[]{:S(2)}) collective-permute-start(bf16[128,1152]{1,0:T(8,128)(2,1)S(1)} %collective-permute-done.11), channel_id=1, source_target_pairs={{1,2},{2,1},{5,6},{6,5},{9,10},{10,9},{13,14},{14,13},{17,18},{18,... | collective-permute-start | bytes 884744 | tf_op jit(solution)/shard_map/ppermute | solution.py:131
  71.3 1.9 %collective-permute-start.9 = (bf16[128,1152]{1,0:T(8,128)(2,1)S(1)}, bf16[128,1152]{1,0:T(8,128)(2,1)S(1)}, u32[]{:S(2)}, u32[]{:S(2)}) collective-permute-start(bf16[128,1152]{1,0:T(8,128)(2,1)S(1)} %collective-permute-done.8), channel_id=1, source_target_pairs={{1,2},{2,1},{5,6},{6,5},{9,10},{10,9},{13,14},{14,13},{17,18},{18,... | collective-permute-start | bytes 884744 | tf_op jit(solution)/shard_map/ppermute | solution.py:131
  72.1 1.6 %collective-permute-start.2 = (bf16[128,1280]{1,0:T(8,128)(2,1)S(1)}, bf16[128,1280]{1,0:T(8,128)(2,1)S(1)}, u32[]{:S(2)}, u32[]{:S(2)}) collective-permute-start(bf16[128,1280]{1,0:T(8,128)(2,1)S(1)} %collective-permute-done.1), channel_id=1, source_target_pairs={{1,2},{2,1},{5,6},{6,5},{9,10},{10,9},{13,14},{14,13},{17,18},{18,... | collective-permute-start | bytes 983048 | tf_op jit(solution)/shard_map/ppermute | solution.py:131
  74.7 36.3 %collective-permute-start.15 = (bf16[448,128]{1,0:T(8,128)(2,1)S(1)}, bf16[448,128]{1,0:T(8,128)(2,1)S(1)}, u32[]{:S(2)}, u32[]{:S(2)}) collective-permute-start(bf16[448,128]{1,0:T(8,128)(2,1)S(1)} %convolution_convert_fusion.3), channel_id=1, source_target_pairs={{1,0},{2,3},{5,4},{6,7},{9,8},{10,11},{13,12},{14,15},{17,16},{18,... | collective-permute-start | bytes 344072 | tf_op jit(solution)/shard_map/ppermute | solution.py:163
  77.5 33.8 %collective-permute-start.13 = (bf16[448,128]{1,0:T(8,128)(2,1)S(1)}, bf16[448,128]{1,0:T(8,128)(2,1)S(1)}, u32[]{:S(2)}, u32[]{:S(2)}) collective-permute-start(bf16[448,128]{1,0:T(8,128)(2,1)S(1)} %add_convert_fusion), channel_id=1, source_target_pairs={{1,0},{2,3},{5,4},{6,7},{9,8},{10,11},{13,12},{14,15},{17,16},{18,... | collective-permute-start | bytes 344072 | tf_op jit(solution)/shard_map/ppermute | solution.py:170
  82.6 28.4 %collective-permute-start.17 = (bf16[448,128]{1,0:T(8,128)(2,1)S(1)}, bf16[448,128]{1,0:T(8,128)(2,1)S(1)}, u32[]{:S(2)}, u32[]{:S(2)}) collective-permute-start(bf16[448,128]{1,0:T(8,128)(2,1)S(1)} %convolution_convert_fusion.2), channel_id=1, source_target_pairs={{1,0},{2,3},{5,4},{6,7},{9,8},{10,11},{13,12},{14,15},{17,16},{18,... | collective-permute-start | bytes 344072 | tf_op jit(solution)/shard_map/ppermute | solution.py:166

commit v3 on v2

--- a/solution.py
+++ b/solution.py
@@ -16,7 +16,7 @@
 
 def spans_of(dim, count):
     lanes = dim // 128
-    edges = [128 * (lanes * at // count) for at in range(count)] + [dim]
+    edges = [128 * -(-lanes * at // count) for at in range(count)] + [dim]
     return [slice(a, b) for a, b in zip(edges, edges[1:])]
 
 
@@ -134,9 +134,9 @@
     while distance < copies:
         gain = gain + lax.ppermute(gain, "dp", swap("dp", distance))
         distance *= 2
-    for route in (inward, across):
-        moved = lax.ppermute(gain, "shard", route)
-        gain = gain + moved
+    routes = (inward, both([(0, 2)]), across)
+    summed = [lax.ppermute(gain, "shard", route) for route in routes]
+    gain = functools.reduce(jnp.add, summed, gain)
     gain_out = lax.ppermute(gain, "shard", outward)
 
     distance = copies // 2
@@ -161,11 +161,12 @@
     edge["far"] = total(whole(edge_weight, far))
     local = total(parts(weight, outer))
     one = lax.ppermute(edge["far"], "shard", outward)
-    near, edge["far"] = lax.optimization_barrier((near, edge["far"]))
+    tail[:-1], edge["far"] = lax.optimization_barrier((tail[:-1], edge["far"]))
+    begun = parts(edge_weight, tail[:-1])
+    near, begun = lax.optimization_barrier((near, begun))
     edge["near"] = dot(edge_weight, near).astype(bf16)
     two = lax.ppermute(edge["near"], "shard", outward)
-    begun = parts(edge_weight, tail[:-1])
-    tail[-1], begun = lax.optimization_barrier((tail[-1], begun))
+    tail[-1], edge["near"] = lax.optimization_barrier((tail[-1], edge["near"]))
     edge["tail"] = total(begun + [dot(edge_weight[:, spans[-1]], tail[-1])])
     three = lax.ppermute(edge["tail"], "shard", outward)
     far, rim, near, tail, _ = lax.optimization_barrier((far, rim, near, tail, edge["tail"]))

time: 113 us -> 102 us (0.903)
  waiting for transfers between devices: 51.7 us -> 43.9 us
  starting transfers between devices: 41.2 us -> 38.5 us
    ppermute x1, waiting for transfers between devices: 26.2 us -> 15 us  [relay(): two = lax.ppermute(edge['near'], 'shard', outward)]
    ppermute x1, starting transfers between devices: 9.17 us -> 4.59 us  [relay(): pieces.append((0, cut, lax.ppermute(piece, 'shard', inward)))]
    ppermute x3, waiting for transfers between devices: 5.81 us -> 9.01 us  [relay(): outer = [lax.ppermute(chunk, other, ends) for chunk in chunks]]
    ppermute x2 -> x3, starting transfers between devices: 4.64 us -> 6.95 us  [relay(): summed = [lax.ppermute(gain, 'shard', route) for route in routes]]
    ppermute x1, waiting for transfers between devices: 0.01 us -> 1.37 us  [relay(): three = lax.ppermute(edge['tail'], 'shard', outward)]
  transfers between devices with their start and end apart: 23 -> 24, of which waited for: 8 -> 8; matrix products, arithmetic and copies ran while one was open for 11% -> 13% of each run, Pallas kernels for 0% -> 0%
where the time goes in v3:
time: 102 us
  waiting for transfers between devices  43.9 us (43%)
  starting transfers between devices  38.5 us (38%)
  matrix products  10.5 us (10%)
  Pallas kernels  3.7 us (4%)
  other arithmetic  2.58 us (3%)
  local copies, waits for them, and re-layouts  1.48 us (1%)
  between operations  1.18 us (1%)
    ppermute x1, waiting for transfers between devices, relay(): two = lax.ppermute(edge['near'], 'shard', outward)  15 us
    ppermute x3, waiting for transfers between devices, relay(): lax.ppermute(block, 'dp', swap('dp', distance))  14.9 us
    dot_general x16, matrix products, dot(): lax.dot_general(w, t, (((1,), (1,)), ((), ())), preferred_element_type=jn...  10.5 us
    ppermute x3, starting transfers between devices, relay(): outer = [lax.ppermute(chunk, other, ends) for chunk in chunks]  9.24 us
    ppermute x3, waiting for transfers between devices, relay(): outer = [lax.ppermute(chunk, other, ends) for chunk in chunks]  9.01 us
    ppermute x3, starting transfers between devices, relay(): summed = [lax.ppermute(gain, 'shard', route) for route in routes]  6.95 us
    ppermute x1, starting transfers between devices, relay(): pieces.append((0, cut, lax.ppermute(piece, 'shard', inward)))  4.59 us
    ppermute x3, starting transfers between devices, relay(): rim = [lax.ppermute(chunk, 'shard', inward) for chunk in outer]  4.05 us
  transfers between devices with their start and end apart: 24, of which 8 were waited for; matrix products, arithmetic and copies ran while one was open for 13% of the time, Pallas kernels for 0%

profile of v3, /device:TPU:0, one launch (start us, length us, event | category | flops | bytes accessed | tf_op | source)
XLA Modules:
  0.0 101.8 jit_solution(16381950865401456178)
XLA Ops:
  0.6 3.7 %norm_backward.1 = (bf16[128,3584]{1,0:T(8,128)(2,1)}, bf16[128,1280]{1,0:T(8,128)(2,1)}, bf16[128,1152]{1,0:T(8,128)(2,1)}, bf16[128,1152]{1,0:T(8,128)(2,1)}, f32[1,3584]{1,0:T(1,128)}) custom-call(bf16[128,3584]{1,0:T(8,128)(2,1)} %bitcast.106, f32[1,3584]{1,0:T(1,128)} %gain_ref.1, bf16[128,3584]{1,0:T(8,128)(2,1)} %bitcast.107, bf16[128,3584]{1,0:T(8,128)(2,1)} %bitcast.108), custom_call_target="tpu_custom_call" | custom-call | flops 5505024 | bytes 4587520 | tf_op jit(solution)/shard_map/norm_backward/pallas_call | solution.py:73
  4.9 1.0 %collective-permute-done.18 = f32[1,3584]{1,0:T(1,128)S(1)} collective-permute-done((f32[1,3584]{1,0:T(1,128)}, f32[1,3584]{1,0:T(1,128)S(1)}, u32[]{:S(2)}, u32[]{:S(2)}) %collective-permute-start.18) | collective-permute-done | bytes 14368 | tf_op jit(solution)/shard_map/ppermute | solution.py:135
  6.0 0.7 add.57
  6.7 2.9 %collective-permute-start.19 = (f32[1,3584]{1,0:T(1,128)S(1)}, f32[1,3584]{1,0:T(1,128)S(1)}, u32[]{:S(2)}, u32[]{:S(2)}) collective-permute-start(f32[1,3584]{1,0:T(1,128)S(1)} %add.57), channel_id=1, source_target_pairs={{0,8},{4,12},{8,0},{12,4},{1,9},{5,13},{9,1},{13,5},{2,10},{6,14},... | collective-permute-start | bytes 43016 | tf_op jit(solution)/shard_map/ppermute | solution.py:135
  9.6 1.7 %collective-permute-done.19 = f32[1,3584]{1,0:T(1,128)S(1)} collective-permute-done((f32[1,3584]{1,0:T(1,128)S(1)}, f32[1,3584]{1,0:T(1,128)S(1)}, u32[]{:S(2)}, u32[]{:S(2)}) %collective-permute-start.19) | collective-permute-done | bytes 14368 | tf_op jit(solution)/shard_map/ppermute | solution.py:135
  11.3 4.0 %collective-permute-start.20 = (f32[1,3584]{1,0:T(1,128)S(1)}, f32[1,3584]{1,0:T(1,128)S(1)}, u32[]{:S(2)}, u32[]{:S(2)}) collective-permute-start(f32[1,3584]{1,0:T(1,128)S(1)} %add.58), channel_id=1, source_target_pairs={{0,1},{3,2},{4,5},{7,6},{8,9},{11,10},{12,13},{15,14},{16,17},{19,... | collective-permute-start | bytes 43016 | tf_op jit(solution)/shard_map/ppermute | solution.py:138
  15.3 2.3 %collective-permute-start.21 = (f32[1,3584]{1,0:T(1,128)S(1)}, f32[1,3584]{1,0:T(1,128)S(1)}, u32[]{:S(2)}, u32[]{:S(2)}) collective-permute-start(f32[1,3584]{1,0:T(1,128)S(1)} %add.58), channel_id=1, source_target_pairs={{0,2},{3,1},{4,6},{7,5},{8,10},{11,9},{12,14},{15,13},{16,18},{19,... | collective-permute-start | bytes 43016 | tf_op jit(solution)/shard_map/ppermute | solution.py:138
  18.3 0.7 collective-permute-done.21
  19.1 1.3 %collective-permute-start.23 = (f32[1,3584]{1,0:T(1,128)S(1)}, f32[1,3584]{1,0:T(1,128)S(1)}, u32[]{:S(2)}, u32[]{:S(2)}) collective-permute-start(f32[1,3584]{1,0:T(1,128)S(1)} %add_add_fusion), channel_id=1, source_target_pairs={{1,0},{2,3},{5,4},{6,7},{9,8},{10,11},{13,12},{14,15},{17,16},{18,... | collective-permute-start | bytes 43016 | tf_op jit(solution)/shard_map/ppermute | solution.py:140
  20.4 1.2 %dynamic-slice_bitcast_fusion = bf16[112,3584]{1,0:T(8,128)(2,1)S(1)} fusion(bf16[1,448,3584]{2,1,0:T(8,128)(2,1)} %param.9, s32[]{:T(128)S(6)} %select_n.83), kind=kLoop, calls=%fused_computation.28 | loop fusion | bytes 1605636 | tf_op jit(solution)/shard_map/dynamic_slice | solution.py:119
  21.6 4.6 %collective-permute-start.1 = (bf16[112,3584]{1,0:T(8,128)(2,1)S(1)}, bf16[112,3584]{1,0:T(8,128)(2,1)S(1)}, u32[]{:S(2)}, u32[]{:S(2)}) collective-permute-start(bf16[112,3584]{1,0:T(8,128)(2,1)S(1)} %dynamic-slice_bitcast_fusion), channel_id=1, source_target_pairs={{0,1},{3,2},{4,5},{7,6},{8,9},{11,10},{12,13},{15,14},{16,17},{19,... | collective-permute-start | bytes 2408456 | tf_op jit(solution)/shard_map/ppermute | solution.py:120
  26.2 0.7 collective-permute-start.11
  26.9 3.4 %collective-permute-start.5 = (bf16[128,1280]{1,0:T(8,128)(2,1)}, bf16[128,1280]{1,0:T(8,128)(2,1)S(1)}, u32[]{:S(2)}, u32[]{:S(2)}) collective-permute-start(bf16[128,1280]{1,0:T(8,128)(2,1)} %get-tuple-element.42), channel_id=1, source_target_pairs={{16,0},{19,3},{0,16},{3,19},{20,4},{23,7},{4,20},{7,23},{24,8},{27... | collective-permute-start | bytes 983048 | tf_op jit(solution)/shard_map/ppermute | solution.py:129
  30.3 2.4 %collective-permute-start.8 = (bf16[128,1152]{1,0:T(8,128)(2,1)}, bf16[128,1152]{1,0:T(8,128)(2,1)S(1)}, u32[]{:S(2)}, u32[]{:S(2)}) collective-permute-start(bf16[128,1152]{1,0:T(8,128)(2,1)} %get-tuple-element.43), channel_id=1, source_target_pairs={{16,0},{19,3},{0,16},{3,19},{20,4},{23,7},{4,20},{7,23},{24,8},{27... | collective-permute-start | bytes 884744 | tf_op jit(solution)/shard_map/ppermute | solution.py:129
  32.8 3.4 %collective-permute-start.12 = (bf16[128,1152]{1,0:T(8,128)(2,1)}, bf16[128,1152]{1,0:T(8,128)(2,1)S(1)}, u32[]{:S(2)}, u32[]{:S(2)}) collective-permute-start(bf16[128,1152]{1,0:T(8,128)(2,1)} %get-tuple-element.48), channel_id=1, source_target_pairs={{16,0},{19,3},{0,16},{3,19},{20,4},{23,7},{4,20},{7,23},{24,8},{27... | collective-permute-start | bytes 884744 | tf_op jit(solution)/shard_map/ppermute | solution.py:129
  36.8 8.9 %collective-permute-done.8 = bf16[128,1152]{1,0:T(8,128)(2,1)S(1)} collective-permute-done((bf16[128,1152]{1,0:T(8,128)(2,1)}, bf16[128,1152]{1,0:T(8,128)(2,1)S(1)}, u32[]{:S(2)}, u32[]{:S(2)}) %collective-permute-start.8) | collective-permute-done | bytes 294944 | tf_op jit(solution)/shard_map/ppermute | solution.py:129
  45.7 1.3 %collective-permute-start.9 = (bf16[128,1152]{1,0:T(8,128)(2,1)S(1)}, bf16[128,1152]{1,0:T(8,128)(2,1)S(1)}, u32[]{:S(2)}, u32[]{:S(2)}) collective-permute-start(bf16[128,1152]{1,0:T(8,128)(2,1)S(1)} %collective-permute-done.8), channel_id=1, source_target_pairs={{0,1},{3,2},{4,5},{7,6},{8,9},{11,10},{12,13},{15,14},{16,17},{19,... | collective-permute-start | bytes 884744 | tf_op jit(solution)/shard_map/ppermute | solution.py:130
  47.0 1.7 %fusion.26 = f32[128,448]{0,1:T(8,128)S(1)} fusion(bf16[128,1152]{1,0:T(8,128)(2,1)S(1)} %collective-permute-done.8, bf16[448,3584]{1,0:T(8,128)(2,1)} %bitcast.94), kind=kOutput, calls=%fused_computation.35 | convolution fusion | flops 132120576 | bytes 1556480 | tf_op jit(solution)/shard_map/dot_general | solution.py:88
  48.9 1.5 %collective-permute-start.3 = (bf16[112,3584]{1,0:T(8,128)(2,1)S(1)}, bf16[112,3584]{1,0:T(8,128)(2,1)S(1)}, u32[]{:S(2)}, u32[]{:S(2)}) collective-permute-start(bf16[112,3584]{1,0:T(8,128)(2,1)S(1)} %collective-permute-done.1), channel_id=1, source_target_pairs={{0,8},{4,12},{8,0},{12,4},{1,9},{5,13},{9,1},{13,5},{2,10},{6,14},... | collective-permute-start | bytes 2408456 | tf_op jit(solution)/shard_map/ppermute | solution.py:145
  50.8 1.4 %collective-permute-start.13 = (bf16[128,1152]{1,0:T(8,128)(2,1)S(1)}, bf16[128,1152]{1,0:T(8,128)(2,1)S(1)}, u32[]{:S(2)}, u32[]{:S(2)}) collective-permute-start(bf16[128,1152]{1,0:T(8,128)(2,1)S(1)} %collective-permute-done.12), channel_id=1, source_target_pairs={{0,1},{3,2},{4,5},{7,6},{8,9},{11,10},{12,13},{15,14},{16,17},{19,... | collective-permute-start | bytes 884744 | tf_op jit(solution)/shard_map/ppermute | solution.py:130
  52.8 1.3 %collective-permute-start.6 = (bf16[128,1280]{1,0:T(8,128)(2,1)S(1)}, bf16[128,1280]{1,0:T(8,128)(2,1)S(1)}, u32[]{:S(2)}, u32[]{:S(2)}) collective-permute-start(bf16[128,1280]{1,0:T(8,128)(2,1)S(1)} %collective-permute-done.5), channel_id=1, source_target_pairs={{0,1},{3,2},{4,5},{7,6},{8,9},{11,10},{12,13},{15,14},{16,17},{19,... | collective-permute-start | bytes 983048 | tf_op jit(solution)/shard_map/ppermute | solution.py:130
  54.2 14.9 %collective-permute-done.3 = bf16[112,3584]{1,0:T(8,128)(2,1)S(1)} collective-permute-done((bf16[112,3584]{1,0:T(8,128)(2,1)S(1)}, bf16[112,3584]{1,0:T(8,128)(2,1)S(1)}, u32[]{:S(2)}, u32[]{:S(2)}) %collective-permute-start.3) | collective-permute-done | bytes 802848 | tf_op jit(solution)/shard_map/ppermute | solution.py:145
  72.1 1.0 convolution_convert_fusion.3
  73.1 1.3 %collective-permute-start.16 = (bf16[448,128]{1,0:T(8,128)(2,1)S(1)}, bf16[448,128]{1,0:T(8,128)(2,1)S(1)}, u32[]{:S(2)}, u32[]{:S(2)}) collective-permute-start(bf16[448,128]{1,0:T(8,128)(2,1)S(1)} %convolution_convert_fusion.3), channel_id=1, source_target_pairs={{1,0},{2,3},{5,4},{6,7},{9,8},{10,11},{13,12},{14,15},{17,16},{18,... | collective-permute-start | bytes 344072 | tf_op jit(solution)/shard_map/ppermute | solution.py:163
  75.3 1.0 convolution_convert_fusion.2
  76.3 1.3 %collective-permute-start.17 = (bf16[448,128]{1,0:T(8,128)(2,1)S(1)}, bf16[448,128]{1,0:T(8,128)(2,1)S(1)}, u32[]{:S(2)}, u32[]{:S(2)}) collective-permute-start(bf16[448,128]{1,0:T(8,128)(2,1)S(1)} %convolution_convert_fusion.2), channel_id=1, source_target_pairs={{1,0},{2,3},{5,4},{6,7},{9,8},{10,11},{13,12},{14,15},{17,16},{18,... | collective-permute-start | bytes 344072 | tf_op jit(solution)/shard_map/ppermute | solution.py:168
  78.1 1.3 %collective-permute-start.15 = (bf16[448,128]{1,0:T(8,128)(2,1)S(1)}, bf16[448,128]{1,0:T(8,128)(2,1)S(1)}, u32[]{:S(2)}, u32[]{:S(2)}) collective-permute-start(bf16[448,128]{1,0:T(8,128)(2,1)S(1)} %fusion.3), channel_id=1, source_target_pairs={{1,0},{2,3},{5,4},{6,7},{9,8},{10,11},{13,12},{14,15},{17,16},{18,... | collective-permute-start | bytes 344072 | tf_op jit(solution)/shard_map/ppermute | solution.py:171
  81.2 1.0 fusion.10
  82.1 1.0 fusion.9
  84.1 15.0 %collective-permute-done.17 = bf16[448,128]{1,0:T(8,128)(2,1)S(1)} collective-permute-done((bf16[448,128]{1,0:T(8,128)(2,1)S(1)}, bf16[448,128]{1,0:T(8,128)(2,1)S(1)}, u32[]{:S(2)}, u32[]{:S(2)}) %collective-permute-start.17) | collective-permute-done | bytes 114720 | tf_op jit(solution)/shard_map/ppermute | solution.py:168
  99.4 1.4 %collective-permute-done.15 = bf16[448,128]{1,0:T(8,128)(2,1)S(1)} collective-permute-done((bf16[448,128]{1,0:T(8,128)(2,1)S(1)}, bf16[448,128]{1,0:T(8,128)(2,1)S(1)}, u32[]{:S(2)}, u32[]{:S(2)}) %collective-permute-start.15) | collective-permute-done | bytes 114720 | tf_op jit(solution)/shard_map/ppermute | solution.py:171
  100.9 0.9 fusion.32
  (62 shorter events, 10.3 us)
Async XLA Ops:
  4.3 46.0 %copy-start = (bf16[1,448,3584]{2,1,0:T(8,128)(2,1)S(1)}, bf16[1,448,3584]{2,1,0:T(8,128)(2,1)}, u32[]{:S(2)}) copy-start(bf16[1,448,3584]{2,1,0:T(8,128)(2,1)} %param.9) | copy-start | bytes 9633796
  4.4 1.6 %collective-permute-start.18 = (f32[1,3584]{1,0:T(1,128)}, f32[1,3584]{1,0:T(1,128)S(1)}, u32[]{:S(2)}, u32[]{:S(2)}) collective-permute-start(f32[1,3584]{1,0:T(1,128)} %get-tuple-element.61), channel_id=1, source_target_pairs={{0,4},{4,0},{8,12},{12,8},{1,5},{5,1},{9,13},{13,9},{2,6},{6,2},{1... | collective-permute-start | bytes 43016 | tf_op jit(solution)/shard_map/ppermute | solution.py:135
  6.7 4.6 %collective-permute-start.19 = (f32[1,3584]{1,0:T(1,128)S(1)}, f32[1,3584]{1,0:T(1,128)S(1)}, u32[]{:S(2)}, u32[]{:S(2)}) collective-permute-start(f32[1,3584]{1,0:T(1,128)S(1)} %add.57), channel_id=1, source_target_pairs={{0,8},{4,12},{8,0},{12,4},{1,9},{5,13},{9,1},{13,5},{2,10},{6,14},... | collective-permute-start | bytes 43016 | tf_op jit(solution)/shard_map/ppermute | solution.py:135
  11.3 7.0 %collective-permute-start.20 = (f32[1,3584]{1,0:T(1,128)S(1)}, f32[1,3584]{1,0:T(1,128)S(1)}, u32[]{:S(2)}, u32[]{:S(2)}) collective-permute-start(f32[1,3584]{1,0:T(1,128)S(1)} %add.58), channel_id=1, source_target_pairs={{0,1},{3,2},{4,5},{7,6},{8,9},{11,10},{12,13},{15,14},{16,17},{19,... | collective-permute-start | bytes 43016 | tf_op jit(solution)/shard_map/ppermute | solution.py:138
  15.3 3.7 %collective-permute-start.21 = (f32[1,3584]{1,0:T(1,128)S(1)}, f32[1,3584]{1,0:T(1,128)S(1)}, u32[]{:S(2)}, u32[]{:S(2)}) collective-permute-start(f32[1,3584]{1,0:T(1,128)S(1)} %add.58), channel_id=1, source_target_pairs={{0,2},{3,1},{4,6},{7,5},{8,10},{11,9},{12,14},{15,13},{16,18},{19,... | collective-permute-start | bytes 43016 | tf_op jit(solution)/shard_map/ppermute | solution.py:138
  17.6 1.4 %collective-permute-start.22 = (f32[1,3584]{1,0:T(1,128)S(1)}, f32[1,3584]{1,0:T(1,128)S(1)}, u32[]{:S(2)}, u32[]{:S(2)}) collective-permute-start(f32[1,3584]{1,0:T(1,128)S(1)} %add.58), channel_id=1, source_target_pairs={{1,2},{2,1},{5,6},{6,5},{9,10},{10,9},{13,14},{14,13},{17,18},{18,... | collective-permute-start | bytes 43016 | tf_op jit(solution)/shard_map/ppermute | solution.py:138
  19.1 13.7 %collective-permute-start.23 = (f32[1,3584]{1,0:T(1,128)S(1)}, f32[1,3584]{1,0:T(1,128)S(1)}, u32[]{:S(2)}, u32[]{:S(2)}) collective-permute-start(f32[1,3584]{1,0:T(1,128)S(1)} %add_add_fusion), channel_id=1, source_target_pairs={{1,0},{2,3},{5,4},{6,7},{9,8},{10,11},{13,12},{14,15},{17,16},{18,... | collective-permute-start | bytes 43016 | tf_op jit(solution)/shard_map/ppermute | solution.py:140
  21.6 27.1 %collective-permute-start.1 = (bf16[112,3584]{1,0:T(8,128)(2,1)S(1)}, bf16[112,3584]{1,0:T(8,128)(2,1)S(1)}, u32[]{:S(2)}, u32[]{:S(2)}) collective-permute-start(bf16[112,3584]{1,0:T(8,128)(2,1)S(1)} %dynamic-slice_bitcast_fusion), channel_id=1, source_target_pairs={{0,1},{3,2},{4,5},{7,6},{8,9},{11,10},{12,13},{15,14},{16,17},{19,... | collective-permute-start | bytes 2408456 | tf_op jit(solution)/shard_map/ppermute | solution.py:120
  26.2 45.9 %collective-permute-start.11 = (bf16[128,3584]{1,0:T(8,128)(2,1)}, bf16[128,3584]{1,0:T(8,128)(2,1)S(1)}, u32[]{:S(2)}, u32[]{:S(2)}) collective-permute-start(bf16[128,3584]{1,0:T(8,128)(2,1)} %get-tuple-element.41), channel_id=1, source_target_pairs={{17,2},{18,1},{1,18},{2,17},{21,6},{22,5},{5,22},{6,21},{25,10},{2... | collective-permute-start | bytes 2752520 | tf_op jit(solution)/shard_map/ppermute | solution.py:127
  26.9 23.9 %collective-permute-start.5 = (bf16[128,1280]{1,0:T(8,128)(2,1)}, bf16[128,1280]{1,0:T(8,128)(2,1)S(1)}, u32[]{:S(2)}, u32[]{:S(2)}) collective-permute-start(bf16[128,1280]{1,0:T(8,128)(2,1)} %get-tuple-element.42), channel_id=1, source_target_pairs={{16,0},{19,3},{0,16},{3,19},{20,4},{23,7},{4,20},{7,23},{24,8},{27... | collective-permute-start | bytes 983048 | tf_op jit(solution)/shard_map/ppermute | solution.py:129
  30.3 15.4 %collective-permute-start.8 = (bf16[128,1152]{1,0:T(8,128)(2,1)}, bf16[128,1152]{1,0:T(8,128)(2,1)S(1)}, u32[]{:S(2)}, u32[]{:S(2)}) collective-permute-start(bf16[128,1152]{1,0:T(8,128)(2,1)} %get-tuple-element.43), channel_id=1, source_target_pairs={{16,0},{19,3},{0,16},{3,19},{20,4},{23,7},{4,20},{7,23},{24,8},{27... | collective-permute-start | bytes 884744 | tf_op jit(solution)/shard_map/ppermute | solution.py:129
  32.8 16.1 %collective-permute-start.12 = (bf16[128,1152]{1,0:T(8,128)(2,1)}, bf16[128,1152]{1,0:T(8,128)(2,1)S(1)}, u32[]{:S(2)}, u32[]{:S(2)}) collective-permute-start(bf16[128,1152]{1,0:T(8,128)(2,1)} %get-tuple-element.48), channel_id=1, source_target_pairs={{16,0},{19,3},{0,16},{3,19},{20,4},{23,7},{4,20},{7,23},{24,8},{27... | collective-permute-start | bytes 884744 | tf_op jit(solution)/shard_map/ppermute | solution.py:129
  45.7 23.5 %collective-permute-start.9 = (bf16[128,1152]{1,0:T(8,128)(2,1)S(1)}, bf16[128,1152]{1,0:T(8,128)(2,1)S(1)}, u32[]{:S(2)}, u32[]{:S(2)}) collective-permute-start(bf16[128,1152]{1,0:T(8,128)(2,1)S(1)} %collective-permute-done.8), channel_id=1, source_target_pairs={{0,1},{3,2},{4,5},{7,6},{8,9},{11,10},{12,13},{15,14},{16,17},{19,... | collective-permute-start | bytes 884744 | tf_op jit(solution)/shard_map/ppermute | solution.py:130
  48.7 4.2 %collective-permute-start.2 = (bf16[112,3584]{1,0:T(8,128)(2,1)S(1)}, bf16[112,3584]{1,0:T(8,128)(2,1)S(1)}, u32[]{:S(2)}, u32[]{:S(2)}) collective-permute-start(bf16[112,3584]{1,0:T(8,128)(2,1)S(1)} %collective-permute-done.1), channel_id=1, source_target_pairs={{0,4},{4,0},{8,12},{12,8},{1,5},{5,1},{9,13},{13,9},{2,6},{6,2},{1... | collective-permute-start | bytes 2408456 | tf_op jit(solution)/shard_map/ppermute | solution.py:145
  48.9 20.2 %collective-permute-start.3 = (bf16[112,3584]{1,0:T(8,128)(2,1)S(1)}, bf16[112,3584]{1,0:T(8,128)(2,1)S(1)}, u32[]{:S(2)}, u32[]{:S(2)}) collective-permute-start(bf16[112,3584]{1,0:T(8,128)(2,1)S(1)} %collective-permute-done.1), channel_id=1, source_target_pairs={{0,8},{4,12},{8,0},{12,4},{1,9},{5,13},{9,1},{13,5},{2,10},{6,14},... | collective-permute-start | bytes 2408456 | tf_op jit(solution)/shard_map/ppermute | solution.py:145
  50.8 18.4 %copy-start.1 = (bf16[128,3584]{1,0:T(8,128)(2,1)S(1)}, bf16[128,3584]{1,0:T(8,128)(2,1)}, u32[]{:S(2)}) copy-start(bf16[128,3584]{1,0:T(8,128)(2,1)} %get-tuple-element.41) | copy-start | bytes 2752516
  50.8 19.1 %collective-permute-start.13 = (bf16[128,1152]{1,0:T(8,128)(2,1)S(1)}, bf16[128,1152]{1,0:T(8,128)(2,1)S(1)}, u32[]{:S(2)}, u32[]{:S(2)}) collective-permute-start(bf16[128,1152]{1,0:T(8,128)(2,1)S(1)} %collective-permute-done.12), channel_id=1, source_target_pairs={{0,1},{3,2},{4,5},{7,6},{8,9},{11,10},{12,13},{15,14},{16,17},{19,... | collective-permute-start | bytes 884744 | tf_op jit(solution)/shard_map/ppermute | solution.py:130
  52.8 17.8 %collective-permute-start.6 = (bf16[128,1280]{1,0:T(8,128)(2,1)S(1)}, bf16[128,1280]{1,0:T(8,128)(2,1)S(1)}, u32[]{:S(2)}, u32[]{:S(2)}) collective-permute-start(bf16[128,1280]{1,0:T(8,128)(2,1)S(1)} %collective-permute-done.5), channel_id=1, source_target_pairs={{0,1},{3,2},{4,5},{7,6},{8,9},{11,10},{12,13},{15,14},{16,17},{19,... | collective-permute-start | bytes 983048 | tf_op jit(solution)/shard_map/ppermute | solution.py:130
  69.1 2.3 %collective-permute-start.4 = (bf16[112,3584]{1,0:T(8,128)(2,1)S(1)}, bf16[112,3584]{1,0:T(8,128)(2,1)S(1)}, u32[]{:S(2)}, u32[]{:S(2)}) collective-permute-start(bf16[112,3584]{1,0:T(8,128)(2,1)S(1)} %collective-permute-done.3), channel_id=1, source_target_pairs={{0,4},{4,0},{8,12},{12,8},{1,5},{5,1},{9,13},{13,9},{2,6},{6,2},{1... | collective-permute-start | bytes 2408456 | tf_op jit(solution)/shard_map/ppermute | solution.py:145
  69.2 6.1 %collective-permute-start = (bf16[128,3584]{1,0:T(8,128)(2,1)S(1)}, bf16[128,3584]{1,0:T(8,128)(2,1)S(1)}, u32[]{:S(2)}, u32[]{:S(2)}) collective-permute-start(bf16[128,3584]{1,0:T(8,128)(2,1)S(1)} %copy-done.1), channel_id=1, source_target_pairs={{17,1},{18,2},{1,17},{2,18},{21,5},{22,6},{5,21},{6,22},{25,9},{26... | collective-permute-start | bytes 2752520 | tf_op jit(solution)/shard_map/ppermute | solution.py:128
  69.9 4.5 %collective-permute-start.10 = (bf16[128,1152]{1,0:T(8,128)(2,1)S(1)}, bf16[128,1152]{1,0:T(8,128)(2,1)S(1)}, u32[]{:S(2)}, u32[]{:S(2)}) collective-permute-start(bf16[128,1152]{1,0:T(8,128)(2,1)S(1)} %collective-permute-done.9), channel_id=1, source_target_pairs={{1,2},{2,1},{5,6},{6,5},{9,10},{10,9},{13,14},{14,13},{17,18},{18,... | collective-permute-start | bytes 884744 | tf_op jit(solution)/shard_map/ppermute | solution.py:131
  70.6 7.0 %collective-permute-start.14 = (bf16[128,1152]{1,0:T(8,128)(2,1)S(1)}, bf16[128,1152]{1,0:T(8,128)(2,1)S(1)}, u32[]{:S(2)}, u32[]{:S(2)}) collective-permute-start(bf16[128,1152]{1,0:T(8,128)(2,1)S(1)} %collective-permute-done.13), channel_id=1, source_target_pairs={{1,2},{2,1},{5,6},{6,5},{9,10},{10,9},{13,14},{14,13},{17,18},{18,... | collective-permute-start | bytes 884744 | tf_op jit(solution)/shard_map/ppermute | solution.py:131
  71.4 3.1 %collective-permute-start.7 = (bf16[128,1280]{1,0:T(8,128)(2,1)S(1)}, bf16[128,1280]{1,0:T(8,128)(2,1)S(1)}, u32[]{:S(2)}, u32[]{:S(2)}) collective-permute-start(bf16[128,1280]{1,0:T(8,128)(2,1)S(1)} %collective-permute-done.6), channel_id=1, source_target_pairs={{1,2},{2,1},{5,6},{6,5},{9,10},{10,9},{13,14},{14,13},{17,18},{18,... | collective-permute-start | bytes 983048 | tf_op jit(solution)/shard_map/ppermute | solution.py:131
  73.1 26.0 %collective-permute-start.16 = (bf16[448,128]{1,0:T(8,128)(2,1)S(1)}, bf16[448,128]{1,0:T(8,128)(2,1)S(1)}, u32[]{:S(2)}, u32[]{:S(2)}) collective-permute-start(bf16[448,128]{1,0:T(8,128)(2,1)S(1)} %convolution_convert_fusion.3), channel_id=1, source_target_pairs={{1,0},{2,3},{5,4},{6,7},{9,8},{10,11},{13,12},{14,15},{17,16},{18,... | collective-permute-start | bytes 344072 | tf_op jit(solution)/shard_map/ppermute | solution.py:163
  76.3 22.8 %collective-permute-start.17 = (bf16[448,128]{1,0:T(8,128)(2,1)S(1)}, bf16[448,128]{1,0:T(8,128)(2,1)S(1)}, u32[]{:S(2)}, u32[]{:S(2)}) collective-permute-start(bf16[448,128]{1,0:T(8,128)(2,1)S(1)} %convolution_convert_fusion.2), channel_id=1, source_target_pairs={{1,0},{2,3},{5,4},{6,7},{9,8},{10,11},{13,12},{14,15},{17,16},{18,... | collective-permute-start | bytes 344072 | tf_op jit(solution)/shard_map/ppermute | solution.py:168
  78.1 22.7 %collective-permute-start.15 = (bf16[448,128]{1,0:T(8,128)(2,1)S(1)}, bf16[448,128]{1,0:T(8,128)(2,1)S(1)}, u32[]{:S(2)}, u32[]{:S(2)}) collective-permute-start(bf16[448,128]{1,0:T(8,128)(2,1)S(1)} %fusion.3), channel_id=1, source_target_pairs={{1,0},{2,3},{5,4},{6,7},{9,8},{10,11},{13,12},{14,15},{17,16},{18,... | collective-permute-start | bytes 344072 | tf_op jit(solution)/shard_map/ppermute | solution.py:171
